TPU v7x, 512 devices: a whole 4x8x8 slice. The times are simulated.
512 devices in a mesh: grp: 16 (over z, core), bis: 32 (over x, y).
Axes of the slice: x: 4, y: 8, z: 8, core: 2. Of those that a mesh axis runs over, the one named last changes fastest.
Arguments:
- positions: float32 [3, 131072], P(None, ('grp', 'bis')), may hold values from -6 to 6
- masses: float32 [131072], P(('grp', 'bis')), may hold values from 0.5 to 2
- smoothing: float32 [131072], P(('grp', 'bis')), may hold values from 0.3 to 3
- swap_lists: int32 [2, 512, 1], P(None, ('grp', 'bis')), may hold values from 0 to 1, as said below
- send_lists: int32 [512, 16, 1], P(('grp', 'bis')), may hold values from 0 to 1
- send_counts: int32 [512, 16], P(('grp', 'bis')), may hold values from 0 to 1, as said below
- neighbours: int32 [1024, 64, 128], P(('grp', 'bis')), may hold values from 0 to 17
Outputs:
- lengths: float32 [131072], P(('grp', 'bis'))
- density: float32 [131072], P(('grp', 'bis'))
Inputs may be any that keep to these rules, and one draw needn't show every extreme that they name: `swap_lists`: within one level and one slab the 1 listed block positions are distinct. `send_counts`: in every draw some group receives 1 block from every slab of its bis index.
All inputs are finite; a program needn't handle non-finite values.
Results may differ from a plain program's by a relative error of at most 0.0003.
Values sent between devices are 32-bit elements; how exact they have to be, the bound alone decides.
A program may use at most 64 MiB of HBM per device.

v0:
```python
import math

import jax
import jax.numpy as jnp
from jax import lax
from jax.sharding import PartitionSpec as P

BLOCK = 128
ITERS = 3


target_count = 16.0
kernel_norm = math.pi**1.5


def from_partner(value, axis, bit):
    return lax.ppermute(value, axis, [(i, i ^ 1 << bit) for i in range(lax.axis_size(axis))])


def settle(dist_sq, neigh_mass, own_mass, start):
    log_len = jnp.log(start)
    for step in range(ITERS):
        width = jnp.exp(2.0 * log_len)
        weight = neigh_mass * jnp.exp(-dist_sq / width[:, None, :])
        count = own_mass + jnp.sum(weight, axis=1)
        second = jnp.sum(weight * dist_sq, axis=1)
        deriv = 2.0 * second / (width * count)
        miss = jnp.log(count) - jnp.log(target_count * own_mass)
        log_len = log_len + jnp.clip(-miss / jnp.maximum(deriv, 1.0), -0.5, 0.5)
    length = jnp.exp(log_len)
    weight = neigh_mass * jnp.exp(-dist_sq / (length * length)[:, None, :])
    count = own_mass + jnp.sum(weight, axis=1)
    return (length, count / (kernel_norm * length * length * length))


def on_device(positions, masses, smoothing, swap_lists, send_lists, send_counts, neighbours):
    blocks_here = masses.shape[0] // BLOCK
    data = jnp.concatenate([positions, masses[None], smoothing[None]], axis=0)
    blocks = data.reshape(5, blocks_here, BLOCK).transpose(1, 0, 2)
    levels = lax.axis_size("bis").bit_length() - 1
    for level in range(2):
        lists = swap_lists[level, 0]
        outgoing = blocks[lists]
        incoming = from_partner(outgoing, "bis", levels - 1 - level)
        blocks = blocks.at[lists].set(incoming)
    groups = send_lists.shape[1]
    slot_cap = send_lists.shape[2]
    slot_ids = jnp.arange(slot_cap, dtype=jnp.int32)
    chosen = send_lists[0]
    keep = (slot_ids[None, :] < send_counts[0][:, None]).astype(jnp.float32)
    outgoing = blocks[chosen][:, :, :4] * keep[:, :, None, None]
    received = lax.all_to_all(outgoing, "grp", split_axis=0, concat_axis=0, tiled=True)
    lane_ids = jnp.arange(BLOCK, dtype=jnp.int32)[None, None, :]
    step_ids = jnp.arange(neighbours.shape[1], dtype=jnp.int32)[None, :, None]
    index = neighbours * jnp.int32(BLOCK) + (lane_ids + step_ids + jnp.int32(1)) % jnp.int32(BLOCK)
    dist_sq = jnp.zeros(neighbours.shape, jnp.float32)
    pool = jnp.concatenate([blocks[:, :4], received.reshape(groups * slot_cap, 4, BLOCK)], axis=0)
    flat = pool.transpose(1, 0, 2).reshape(4, -1)
    picked = jnp.take(flat, index, axis=1)
    for comp in range(3):
        diff = picked[comp] - blocks[:, comp][:, None, :]
        dist_sq = dist_sq + diff * diff
    neigh_mass = picked[3]
    length, density = settle(dist_sq, neigh_mass, blocks[:, 3], blocks[:, 4])
    return (length.reshape(-1), density.reshape(-1))


def solution(mesh):
    placed = (
        P(None, ("grp", "bis")),
        P(("grp", "bis")),
        P(("grp", "bis")),
        P(None, ("grp", "bis"), None),
        P(("grp", "bis"), None, None),
        P(("grp", "bis"), None),
        P(("grp", "bis"), None, None),
    )
    return jax.shard_map(
        on_device,
        mesh=mesh,
        in_specs=placed,
        out_specs=(P(("grp", "bis")), P(("grp", "bis"))),
        check_vma=False,
    )
```

profile of v0, /device:TPU:1, one launch (start us, length us, event | category | flops | bytes accessed | tf_op | source)
XLA Modules:
  0.0 105.0 jit_solution(14722010203483940521)
XLA Ops:
  0.6 1.3 %fusion.25 = (s32[1,1,1]{0,2,1:T(1,128)}, s32[1,1,1]{0,2,1:T(1,128)}) fusion(s32[2,1,1]{0,2,1:T(1,128)} %param.14), kind=kLoop, calls=%fused_computation.95 | loop fusion | bytes 16 | tf_op jit(solution)/shard_map/slice | solution.py:42
  3.2 0.7 concatenate.21
  4.6 0.7 pad_maximum_fusion
  5.3 5.5 %collective-permute-start = (f32[1,5,128]{2,0,1:T(1,128)S(1)}, f32[1,5,128]{2,0,1:T(1,128)S(1)}, u32[]{:S(2)}, u32[]{:S(2)}) collective-permute-start(f32[1,5,128]{2,0,1:T(1,128)S(1)} %dynamic-slice_bitcast_fusion), channel_id=1, source_target_pairs={{0,16},{1,17},{2,18},{3,19},{4,20},{5,21},{6,22},{7,23},{8,24},{9,... | collective-permute-start | bytes 7688 | tf_op jit(solution)/shard_map/ppermute | solution.py:17
  12.1 0.7 fusion.23
  12.8 0.7 fusion.22
  13.4 0.9 compare_and_fusion
  15.0 1.5 %and_reduce_fusion = (pred[]{:T(512)}, pred[]{:T(512)}) fusion(s32[3]{0:T(128)} %constant.80.clone.1, s32[1]{0:T(128)} %constant.78.clone.1, s32[1]{0:T(128)} %select_n.42, s32[1]{0:T(128)} %select_n.41), kind=kLoop, calls=%fused_computation.42 | loop fusion | flops 34 | bytes 26 | tf_op jit(solution)/shard_map/reduce.3
  16.4 0.7 fusion.26
  17.1 0.0 collective-permute-done
  17.1 0.6 broadcast_select_fusion.1
  17.8 2.2 %collective-permute-start.1 = (f32[1,5,128]{2,0,1:T(1,128)S(1)}, f32[1,5,128]{2,0,1:T(1,128)S(1)}, u32[]{:S(2)}, u32[]{:S(2)}) collective-permute-start(f32[1,5,128]{2,0,1:T(1,128)S(1)} %constant_dynamic-slice_fusion), channel_id=1, source_target_pairs={{0,8},{1,9},{2,10},{3,11},{4,12},{5,13},{6,14},{7,15},{8,0},{9,1},... | collective-permute-start | bytes 7688 | tf_op jit(solution)/shard_map/ppermute | solution.py:17
  20.0 2.1 %collective-permute-done.1 = f32[1,5,128]{2,0,1:T(1,128)S(1)} collective-permute-done((f32[1,5,128]{2,0,1:T(1,128)S(1)}, f32[1,5,128]{2,0,1:T(1,128)S(1)}, u32[]{:S(2)}, u32[]{:S(2)}) %collective-permute-start.1) | collective-permute-done | bytes 2592 | tf_op jit(solution)/shard_map/ppermute | solution.py:17
  22.1 0.7 broadcast_select_fusion
  22.8 0.6 gather_fusion
  23.4 0.1 slice_multiply_fusion
  23.5 0.6 copy.46
  24.1 12.4 %all-to-all-start = ((f32[16,1,4,128]{3,2,1,0:T(4,128)}), f32[16,1,4,128]{3,2,1,0:T(4,128)S(1)}, u32[]{:S(2)}, u32[]{:S(2)}) async-start(f32[16,1,4,128]{3,2,1,0:T(4,128)} %copy.46), calls=%async_computation | async-start | bytes 65536 | tf_op jit(solution)/shard_map/all_to_all | solution.py:52
  36.6 7.4 %all-to-all-done = f32[16,1,4,128]{3,2,1,0:T(4,128)S(1)} async-done(((f32[16,1,4,128]{3,2,1,0:T(4,128)}), f32[16,1,4,128]{3,2,1,0:T(4,128)S(1)}, u32[]{:S(2)}, u32[]{:S(2)}) %all-to-all-start) | async-done | bytes 32800 | tf_op jit(solution)/shard_map/all_to_all | solution.py:52
  44.0 0.4 copy.48
  44.4 54.4 %gather_fusion.1 = f32[16384,4]{1,0:T(8,128)} fusion(f32[4,2304]{0,1:T(8,128)S(1)} %copy.48, s32[16384]{0:T(1024)S(1)} %broadcast_clamp_fusion), kind=kCustom, calls=%fused_computation.1 | custom fusion | bytes 589824 | tf_op jit(solution)/shard_map/jit(_take)/gather | solution.py:59
  98.8 5.2 %copy.49 = f32[2,64,128,4]{2,1,0,3:T(8,128)S(1)} copy(f32[2,64,128,4]{3,2,1,0:T(8,128)} %bitcast.196) | data formatting | bytes 524288 | tf_op jit(solution)/shard_map/jit(_take)/gather | solution.py:59
  104.1 0.1 multiply_reduce_fusion.3
  104.2 0.1 multiply_reduce_fusion.2
  104.2 0.1 multiply_reduce_fusion.1
  104.3 0.1 multiply_reduce_fusion
  104.4 0.7 fusion.12
  (17 shorter events, 0.3 us)
Async XLA Ops:
  5.3 11.8 %collective-permute-start = (f32[1,5,128]{2,0,1:T(1,128)S(1)}, f32[1,5,128]{2,0,1:T(1,128)S(1)}, u32[]{:S(2)}, u32[]{:S(2)}) collective-permute-start(f32[1,5,128]{2,0,1:T(1,128)S(1)} %dynamic-slice_bitcast_fusion), channel_id=1, source_target_pairs={{0,16},{1,17},{2,18},{3,19},{4,20},{5,21},{6,22},{7,23},{8,24},{9,... | collective-permute-start | bytes 7688 | tf_op jit(solution)/shard_map/ppermute | solution.py:17
  17.8 4.3 %collective-permute-start.1 = (f32[1,5,128]{2,0,1:T(1,128)S(1)}, f32[1,5,128]{2,0,1:T(1,128)S(1)}, u32[]{:S(2)}, u32[]{:S(2)}) collective-permute-start(f32[1,5,128]{2,0,1:T(1,128)S(1)} %constant_dynamic-slice_fusion), channel_id=1, source_target_pairs={{0,8},{1,9},{2,10},{3,11},{4,12},{5,13},{6,14},{7,15},{8,0},{9,1},... | collective-permute-start | bytes 7688 | tf_op jit(solution)/shard_map/ppermute | solution.py:17
  24.1 19.8 %all-to-all-start = ((f32[16,1,4,128]{3,2,1,0:T(4,128)}), f32[16,1,4,128]{3,2,1,0:T(4,128)S(1)}, u32[]{:S(2)}, u32[]{:S(2)}) async-start(f32[16,1,4,128]{3,2,1,0:T(4,128)} %copy.46), calls=%async_computation | async-start | bytes 65536 | tf_op jit(solution)/shard_map/all_to_all | solution.py:52
where the time goes:
time: 106 us; the launch traced here: 105 us
  local copies, waits for them, and re-layouts  63.4 us (60%)
  starting transfers between devices  20.1 us (19%)
  waiting for transfers between devices  9.46 us (9%)
  other arithmetic  7.42 us (7%)
  between operations  4.67 us (4%)
    gather x2, local copies, waits for them, and re-layouts, on_device(): picked = jnp.take(flat, index, axis=1)  59.7 us
    all_to_all x1, starting transfers between devices, on_device(): lax.all_to_all(outgoing, 'grp', split_axis=0, concat_axis=0, tiled=True)  12.4 us
    ppermute x2, starting transfers between devices, from_partner(): lax.ppermute(value, axis, [(i, i ^ 1 << bit) for i in range(lax.axis_size...  7.7 us
    all_to_all x1, waiting for transfers between devices, on_device(): lax.all_to_all(outgoing, 'grp', split_axis=0, concat_axis=0, tiled=True)  7.36 us
    another operation x3, other arithmetic  2.72 us
  transfers between devices with their start and end apart: 3, of which 2 were waited for; matrix products, arithmetic and copies ran while one was open for 4% of the time, Pallas kernels for 0%

commit v1 on v0

v1 whole, which is shorter than its diff:
```python
import math

import jax
import jax.numpy as jnp
from jax import lax
from jax.experimental import pallas as pl
from jax.experimental.pallas import tpu as pltpu
from jax.sharding import PartitionSpec as P

BLOCK = 128
ROWS = 8
SENT = 4
ITERS = 3
TARGET = 16.0
NORM = math.pi**-1.5
LOG2E = math.log2(math.e)
MESH = pl.DeviceIdType.MESH


def pick_rows(table, index):
    return jnp.take_along_axis(table, index, axis=0, mode="promise_in_bounds")


def pick_lanes(table, index):
    return jnp.take_along_axis(table, index, axis=1, mode="promise_in_bounds")


def kernel(
    n_grp,
    n_bis,
    knb,
    pos_hbm,
    mass_hbm,
    smooth_hbm,
    swap_hbm,
    list_hbm,
    count_hbm,
    near_hbm,
    length_ref,
    density_ref,
    pos,
    mass,
    smooth,
    swap,
    lists,
    counts,
    near,
    index,
    trade_out,
    trade_in,
    final,
    deliver_out,
    deliver_in,
    moved,
    load_sem,
    trade_send,
    trade_recv,
    deliver_send,
    deliver_recv,
):
    g = lax.axis_index("grp")
    b = lax.axis_index("bis")
    half, quarter = n_bis // 2, n_bis // 4
    first = (b + half) % n_bis
    second = b + quarter - half * ((b // quarter) % 2)
    both = (second + half) % n_bis

    barrier = pltpu.get_barrier_semaphore()
    for partner in (first, second, both):
        pl.semaphore_signal(barrier, inc=1, device_id={"bis": partner}, device_id_type=MESH)
    for j in range(1, n_grp):
        pl.semaphore_signal(barrier, inc=1, device_id={"grp": (g + j) % n_grp}, device_id_type=MESH)

    loads = [
        pltpu.make_async_copy(src, dst, load_sem.at[i])
        for i, (src, dst) in enumerate(
            [
                (near_hbm, near),
                (swap_hbm, swap),
                (pos_hbm, pos),
                (mass_hbm, mass),
                (smooth_hbm, smooth),
                (list_hbm, lists),
                (count_hbm, counts),
            ]
        )
    ]
    for load in loads:
        load.start()
    for load in loads[1:]:
        load.wait()

    l0, l1 = swap[0], swap[1]
    flag = jnp.where(jnp.full((1, BLOCK), l0, jnp.int32) != l1, 1.0, 0.0)
    tail = jnp.zeros((ROWS - 6, BLOCK), jnp.float32)
    for k in range(2):
        lanes = slice(k * BLOCK, (k + 1) * BLOCK)
        final[k] = jnp.concatenate([pos[:, lanes], mass[k : k + 1], smooth[k : k + 1], flag, tail], axis=0)
    blocks = [final[0], final[1]]
    whole = lambda value: jnp.full((ROWS, BLOCK), value, jnp.int32)
    trade_out[0] = jnp.where(whole(l0) == 0, blocks[0], blocks[1])
    trade_out[1] = jnp.where(whole(l1) == 0, blocks[0], blocks[1])

    pl.semaphore_wait(barrier, n_grp - 1 + 3)

    trades = [
        pltpu.make_async_remote_copy(
            src_ref=trade_out.at[src],
            dst_ref=trade_in.at[dst],
            send_sem=trade_send,
            recv_sem=trade_recv,
            device_id={"bis": partner},
            device_id_type=MESH,
        )
        for src, dst, partner in ((0, 0, first), (1, 1, second), (0, 2, both))
    ]
    for trade in trades:
        trade.start()

    loads[0].wait()
    for k in range(2):
        slot = near[k]
        turned = pltpu.roll(slot, 1, 1, stride=1, stride_axis=0)
        index[k] = jnp.where(turned < 2, turned, 2 + ((g + 2 - turned + n_grp) & (n_grp - 1)))

    pltpu.make_async_remote_copy(
        src_ref=trade_in,
        dst_ref=trade_in,
        send_sem=trade_send,
        recv_sem=trade_recv,
        device_id={"bis": first},
        device_id_type=MESH,
    ).wait_recv()

    from_first, from_second, from_both = trade_in[0], trade_in[1], trade_in[2]
    kept = jnp.broadcast_to(from_second[5:6], (ROWS, BLOCK)) != 0.0
    from_second = jnp.where(kept, from_second, from_both)
    for k in range(2):
        block = jnp.where(whole(l0) == k, from_first, blocks[k])
        blocks[k] = jnp.where(whole(l1) == k, from_second, block)
        final[k] = blocks[k]

    delivers = []
    for j in range(n_grp):
        to = (g + j) % n_grp
        block = jnp.where(whole(lists[to]) == 0, blocks[0], blocks[1])
        block = jnp.where(whole(counts[to]) > 0, block, 0.0)
        if j == 0:
            deliver_in[0:SENT] = block[0:SENT]
            continue
        deliver_out[SENT * j : SENT * (j + 1)] = block[0:SENT]
        deliver = pltpu.make_async_remote_copy(
            src_ref=deliver_out.at[pl.ds(SENT * j, SENT)],
            dst_ref=deliver_in.at[pl.ds(SENT * j, SENT)],
            send_sem=deliver_send,
            recv_sem=deliver_recv,
            device_id={"grp": to},
            device_id_type=MESH,
        )
        deliver.start()

    own_rows = [jnp.concatenate([blocks[k][c : c + 1] for k in (0, 1) for _ in range(4)], axis=0) for c in range(4)]
    for k in range(2):
        for c in range(3):
            row = jnp.broadcast_to(blocks[k][c : c + 1], (knb, BLOCK))
            moved[k, c] = pltpu.roll(row, 1, 1, stride=1, stride_axis=0)

    pltpu.make_async_remote_copy(
        src_ref=deliver_in.at[pl.ds(SENT, SENT * (n_grp - 1))],
        dst_ref=deliver_in.at[pl.ds(SENT, SENT * (n_grp - 1))],
        send_sem=deliver_send,
        recv_sem=deliver_recv,
        device_id={"grp": g},
        device_id_type=MESH,
    ).wait_recv()

    low = [deliver_in[pl.ds(c, 8, stride=SENT), :] for c in range(4)]
    high = [deliver_in[pl.ds(8 * SENT + c, 8, stride=SENT), :] for c in range(4)]
    lane = lax.broadcasted_iota(jnp.int32, (8, BLOCK), 1)
    row = lax.broadcasted_iota(jnp.int32, (8, BLOCK), 0)
    dist, weigh = [], []
    for k in range(2):
        dist_rows, mass_rows = [], []
        for v in range(knb // 8):
            where = index[k, 8 * v : 8 * (v + 1), :]
            rel = where - 2
            is_own = where < 2
            is_low = rel < 8
            sub = rel & 7
            own_sub = where * 4 & 7
            comps = []
            for c in range(4):
                got = jnp.where(is_low, pick_rows(low[c], sub), pick_rows(high[c], sub))
                comps.append(jnp.where(is_own, pick_rows(own_rows[c], own_sub), got))
            total = None
            for c in range(3):
                diff = comps[c] - moved[k, c, 8 * v : 8 * (v + 1), :]
                total = diff * diff if total is None else total + diff * diff
            back = (lane + row + (8 * v + 1)) & (BLOCK - 1)
            dist_rows.append(pick_lanes(total, back))
            mass_rows.append(pick_lanes(comps[3], back))
        dist.append(jnp.concatenate(dist_rows, axis=0))
        weigh.append(jnp.concatenate(mass_rows, axis=0))

    for k in range(2):
        own_mass, start = blocks[k][3:4], blocks[k][4:5]
        log_target = jnp.log(TARGET * own_mass)
        length, inverse = start, 1.0 / start
        for step in range(ITERS):
            narrow = inverse * inverse
            weight = weigh[k] * jnp.exp2(dist[k] * (narrow * -LOG2E))
            count = own_mass + jnp.sum(weight, axis=0, keepdims=True)
            second_sum = jnp.sum(weight * dist[k], axis=0, keepdims=True)
            miss = jnp.log(count) - log_target
            move = jnp.clip(-miss * count / jnp.maximum(2.0 * second_sum * narrow, count), -0.5, 0.5)
            length = length * jnp.exp(move)
            inverse = inverse * jnp.exp(-move)
        narrow = inverse * inverse
        weight = weigh[k] * jnp.exp2(dist[k] * (narrow * -LOG2E))
        count = own_mass + jnp.sum(weight, axis=0, keepdims=True)
        length_ref[k : k + 1, :] = length
        density_ref[k : k + 1, :] = count * (NORM * narrow * inverse)

    for trade in trades:
        trade.wait_send()
    pltpu.make_async_remote_copy(
        src_ref=deliver_out.at[pl.ds(SENT, SENT * (n_grp - 1))],
        dst_ref=deliver_out.at[pl.ds(SENT, SENT * (n_grp - 1))],
        send_sem=deliver_send,
        recv_sem=deliver_recv,
        device_id={"grp": g},
        device_id_type=MESH,
    ).wait_send()


def solution(mesh):
    n_grp, n_bis = mesh.shape["grp"], mesh.shape["bis"]

    def on_device(positions, masses, smoothing, swap_lists, send_lists, send_counts, neighbours):
        knb = neighbours.shape[1]
        any_space = pl.BlockSpec(memory_space=pl.ANY)
        vmem = pl.BlockSpec(memory_space=pltpu.VMEM)
        f32, i32 = jnp.float32, jnp.int32
        length, density = pl.pallas_call(
            lambda *refs: kernel(n_grp, n_bis, knb, *refs),
            name="settle",
            out_shape=[jax.ShapeDtypeStruct((2, BLOCK), f32)] * 2,
            in_specs=[any_space] * 7,
            out_specs=[vmem, vmem],
            scratch_shapes=[
                pltpu.VMEM((3, 2 * BLOCK), f32),
                pltpu.VMEM((2, BLOCK), f32),
                pltpu.VMEM((2, BLOCK), f32),
                pltpu.SMEM((2,), i32),
                pltpu.SMEM((n_grp,), i32),
                pltpu.SMEM((n_grp,), i32),
                pltpu.VMEM((2, knb, BLOCK), i32),
                pltpu.VMEM((2, knb, BLOCK), i32),
                pltpu.VMEM((2, ROWS, BLOCK), f32),
                pltpu.VMEM((3, ROWS, BLOCK), f32),
                pltpu.VMEM((2, ROWS, BLOCK), f32),
                pltpu.VMEM((SENT * n_grp, BLOCK), f32),
                pltpu.VMEM((SENT * n_grp, BLOCK), f32),
                pltpu.VMEM((2, 3, knb, BLOCK), f32),
                pltpu.SemaphoreType.DMA((7,)),
                pltpu.SemaphoreType.DMA,
                pltpu.SemaphoreType.DMA,
                pltpu.SemaphoreType.DMA,
                pltpu.SemaphoreType.DMA,
            ],
            compiler_params=pltpu.CompilerParams(collective_id=0, has_side_effects=True, vmem_limit_bytes=4 << 20),
        )(
            positions,
            masses.reshape(2, BLOCK),
            smoothing.reshape(2, BLOCK),
            swap_lists.reshape(2),
            send_lists.reshape(n_grp),
            send_counts.reshape(n_grp),
            neighbours,
        )
        return length.reshape(-1), density.reshape(-1)

    ranks = P(("grp", "bis"))
    placed = (
        P(None, ("grp", "bis")),
        ranks,
        ranks,
        P(None, ("grp", "bis"), None),
        P(("grp", "bis"), None, None),
        P(("grp", "bis"), None),
        P(("grp", "bis"), None, None),
    )
    return jax.shard_map(on_device, mesh=mesh, in_specs=placed, out_specs=(ranks, ranks), check_vma=False)
```

time: 106 us -> 24.6 us (0.23)
  local copies, waits for them, and re-layouts: 63.4 us -> 2.66 us
  Pallas kernels: 0 us -> 21 us
  starting transfers between devices: 20.1 us -> 0 us
  waiting for transfers between devices: 9.46 us -> 0 us
  other arithmetic: 7.42 us -> 0 us
  between operations: 4.67 us -> 0.69 us
    gather x6 -> x0, local copies, waits for them, and re-layouts: 60.2 us -> none  [the longest x2 59.7 us: on_device(): picked = jnp.take(flat, index, axis=1)]
    pallas_call x0 -> x1, Pallas kernels: none -> 21 us  [on_device(): pl.pallas_call(lambda *refs: kernel(n_grp, n_bis, knb, *refs), name='sett...]
    all_to_all x1 -> x0, starting transfers between devices: 12.4 us -> none  [on_device(): lax.all_to_all(outgoing, 'grp', split_axis=0, concat_axis=0, tiled=True)]
    ppermute x2 -> x0, starting transfers between devices: 7.7 us -> none  [from_partner(): lax.ppermute(value, axis, [(i, i ^ 1 << bit) for i in range(lax.axis_size...]
    all_to_all x1 -> x0, waiting for transfers between devices: 7.36 us -> none  [on_device(): lax.all_to_all(outgoing, 'grp', split_axis=0, concat_axis=0, tiled=True)]
    another operation x3 -> x0, other arithmetic: 2.72 us -> none
    unnamed x0 -> x16, local copies, waits for them, and re-layouts: none -> 2.66 us
    ppermute x2 -> x0, waiting for transfers between devices: 2.1 us -> none  [from_partner(): lax.ppermute(value, axis, [(i, i ^ 1 << bit) for i in range(lax.axis_size...]
  transfers between devices with their start and end apart: 3 -> 0, of which waited for: 2 -> 0; matrix products, arithmetic and copies ran while one was open for 4% -> 0% of each run, Pallas kernels for 0% -> 0%
where the time goes in v1:
time: 24.6 us; the launch traced here: 24.4 us
  Pallas kernels  21 us (85%)
  local copies, waits for them, and re-layouts  2.66 us (11%)
  between operations  0.69 us (3%)
    pallas_call x1, Pallas kernels, on_device(): pl.pallas_call(lambda *refs: kernel(n_grp, n_bis, knb, *refs), name='sett...  21 us
    unnamed x16, local copies, waits for them, and re-layouts  2.66 us

profile of v1, /device:TPU:1, one launch (start us, length us, event | category | flops | bytes accessed | tf_op | source)
XLA Modules:
  0.0 24.4 jit_solution(15211409445087825322)
XLA Ops:
  0.6 0.0 copy-start.1
  0.6 0.0 copy-start.3
  0.7 0.0 copy-start.5
  0.7 0.0 copy-start.6
  0.7 0.0 copy-start.2
  0.7 0.0 copy-start.4
  0.7 0.6 %copy-done.1 = f32[3,256]{1,0:T(4,128)S(1)} copy-done((f32[3,256]{1,0:T(4,128)S(1)}, f32[3,256]{1,0:T(4,128)}, u32[]{:S(2)}) %copy-start.1) | copy-done | bytes 3096
  1.3 0.0 copy-done.3
  1.3 0.0 copy-done.5
  1.3 0.0 copy-done.6
  1.3 0.0 copy-done.2
  1.4 0.0 copy-done.4
  1.4 0.0 copy-start
  1.4 0.8 %copy-done = s32[2,64,128]{2,1,0:T(8,128)S(1)} copy-done((s32[2,64,128]{2,1,0:T(8,128)S(1)}, s32[2,64,128]{2,1,0:T(8,128)}, u32[]{:S(2)}) %copy-start) | copy-done | bytes 65560
  2.2 21.0 %settle.1 = (f32[2,128]{1,0:T(2,128)S(1)}, f32[2,128]{1,0:T(2,128)S(1)}) custom-call(f32[3,256]{1,0:T(4,128)S(1)} %copy-done.1, f32[2,128]{1,0:T(2,128)S(1)} %bitcast.7, f32[2,128]{1,0:T(2,128)S(1)} %bitcast.8, s32[2]{0:T(128)S(1)} %bitcast.11, s32[16]{0:T(128)S(1)} %bitcast.12, s32[16]{0:T(128)S(1)} %bitcast.13, s32[2,64,128]{2,1,0:T(8,128)S(1)} %copy-done), custom_call_target="tpu_custom_call" | custom-call | tf_op jit(solution)/shard_map/settle/pallas_call | solution.py:244
  23.3 0.6 %copy.11 = f32[256]{0:T(256)} copy(f32[256]{0:T(256)S(1)} %bitcast.10) | data formatting | bytes 2048
  23.8 0.6 %copy.12 = f32[256]{0:T(256)} copy(f32[256]{0:T(256)S(1)} %bitcast.9) | data formatting | bytes 2048
Async XLA Ops:
  0.6 0.7 %copy-start.1 = (f32[3,256]{1,0:T(4,128)S(1)}, f32[3,256]{1,0:T(4,128)}, u32[]{:S(2)}) copy-start(f32[3,256]{1,0:T(4,128)} %refs_0_.1) | copy-start | bytes 9220
  0.6 0.7 %copy-start.3 = (f32[256]{0:T(256)S(1)}, f32[256]{0:T(256)}, u32[]{:S(2)}) copy-start(f32[256]{0:T(256)} %param.9) | copy-start | bytes 3076
  0.7 0.7 %copy-start.5 = (s32[1,16,1]{1,2,0:T(1,128)S(1)}, s32[1,16,1]{1,2,0:T(1,128)}, u32[]{:S(2)}) copy-start(s32[1,16,1]{1,2,0:T(1,128)} %param.11) | copy-start | bytes 196
  0.7 0.7 %copy-start.6 = (s32[1,16]{1,0:T(1,128)S(1)}, s32[1,16]{1,0:T(1,128)}, u32[]{:S(2)}) copy-start(s32[1,16]{1,0:T(1,128)} %param.12) | copy-start | bytes 196
  0.7 0.7 %copy-start.2 = (f32[256]{0:T(256)S(1)}, f32[256]{0:T(256)}, u32[]{:S(2)}) copy-start(f32[256]{0:T(256)} %param.8) | copy-start | bytes 3076
  0.7 0.7 %copy-start.4 = (s32[2,1,1]{0,2,1:T(1,128)S(1)}, s32[2,1,1]{0,2,1:T(1,128)}, u32[]{:S(2)}) copy-start(s32[2,1,1]{0,2,1:T(1,128)} %param.10) | copy-start | bytes 28
  1.4 0.8 %copy-start = (s32[2,64,128]{2,1,0:T(8,128)S(1)}, s32[2,64,128]{2,1,0:T(8,128)}, u32[]{:S(2)}) copy-start(s32[2,64,128]{2,1,0:T(8,128)} %refs_6_.1) | copy-start | bytes 196612

commit v2 on v1

--- a/solution.py
+++ b/solution.py
@@ -36,8 +36,8 @@
     list_hbm,
     count_hbm,
     near_hbm,
-    length_ref,
-    density_ref,
+    inverse_ref,
+    count_ref,
     pos,
     mass,
     smooth,
@@ -57,6 +57,7 @@
     trade_recv,
     deliver_send,
     deliver_recv,
+    beyond,
 ):
     g = lax.axis_index("grp")
     b = lax.axis_index("bis")
@@ -65,11 +66,23 @@
     second = b + quarter - half * ((b // quarter) % 2)
     both = (second + half) % n_bis
 
+    chips = n_grp // 2
+    chip, core = g // 2, g % 2
+
+    def place(chip_step, core_step):
+        return (chip + chip_step) % chips * 2 + (core + core_step) % 2
+
+    order = sorted(
+        [(step, turn) for step in range(chips) for turn in range(2) if step or turn],
+        key=lambda hop: -min(hop[0], chips - hop[0]),
+    )
+
     barrier = pltpu.get_barrier_semaphore()
     for partner in (first, second, both):
         pl.semaphore_signal(barrier, inc=1, device_id={"bis": partner}, device_id_type=MESH)
-    for j in range(1, n_grp):
-        pl.semaphore_signal(barrier, inc=1, device_id={"grp": (g + j) % n_grp}, device_id_type=MESH)
+    near_hops = [hop for hop in order if min(hop[0], chips - hop[0]) <= 2]
+    for hop in near_hops:
+        pl.semaphore_signal(barrier, inc=1, device_id={"grp": place(*hop)}, device_id_type=MESH)
 
     loads = [
         pltpu.make_async_copy(src, dst, load_sem.at[i])
@@ -101,7 +114,9 @@
     trade_out[0] = jnp.where(whole(l0) == 0, blocks[0], blocks[1])
     trade_out[1] = jnp.where(whole(l1) == 0, blocks[0], blocks[1])
 
-    pl.semaphore_wait(barrier, n_grp - 1 + 3)
+    pl.semaphore_wait(barrier, len(near_hops) + 3)
+    for side, step in enumerate((2, chips - 2)):
+        pl.semaphore_signal(beyond.at[side], inc=1, device_id={"grp": place(step, 0)}, device_id_type=MESH)
 
     trades = [
         pltpu.make_async_remote_copy(
@@ -121,7 +136,9 @@
     for k in range(2):
         slot = near[k]
         turned = pltpu.roll(slot, 1, 1, stride=1, stride_axis=0)
-        index[k] = jnp.where(turned < 2, turned, 2 + ((g + 2 - turned + n_grp) & (n_grp - 1)))
+        source = turned - 2
+        offset = ((2 * chip - (source & -2)) & (n_grp - 1)) + ((core - source) & 1)
+        index[k] = jnp.where(turned < 2, turned, 2 + offset)
 
     pltpu.make_async_remote_copy(
         src_ref=trade_in,
@@ -140,24 +157,25 @@
         blocks[k] = jnp.where(whole(l1) == k, from_second, block)
         final[k] = blocks[k]
 
-    delivers = []
-    for j in range(n_grp):
-        to = (g + j) % n_grp
+    for side in range(2):
+        pl.semaphore_wait(beyond.at[side], 1)
+    for hop in [*order, (0, 0)]:
+        to = place(*hop)
+        slot = pl.ds(SENT * (2 * hop[0] + hop[1]), SENT)
         block = jnp.where(whole(lists[to]) == 0, blocks[0], blocks[1])
         block = jnp.where(whole(counts[to]) > 0, block, 0.0)
-        if j == 0:
-            deliver_in[0:SENT] = block[0:SENT]
+        if hop == (0, 0):
+            deliver_in[slot] = block[0:SENT]
             continue
-        deliver_out[SENT * j : SENT * (j + 1)] = block[0:SENT]
-        deliver = pltpu.make_async_remote_copy(
-            src_ref=deliver_out.at[pl.ds(SENT * j, SENT)],
-            dst_ref=deliver_in.at[pl.ds(SENT * j, SENT)],
+        deliver_out[slot] = block[0:SENT]
+        pltpu.make_async_remote_copy(
+            src_ref=deliver_out.at[slot],
+            dst_ref=deliver_in.at[slot],
             send_sem=deliver_send,
             recv_sem=deliver_recv,
             device_id={"grp": to},
             device_id_type=MESH,
-        )
-        deliver.start()
+        ).start()
 
     own_rows = [jnp.concatenate([blocks[k][c : c + 1] for k in (0, 1) for _ in range(4)], axis=0) for c in range(4)]
     for k in range(2):
@@ -205,7 +223,7 @@
     for k in range(2):
         own_mass, start = blocks[k][3:4], blocks[k][4:5]
         log_target = jnp.log(TARGET * own_mass)
-        length, inverse = start, 1.0 / start
+        inverse = 1.0 / start
         for step in range(ITERS):
             narrow = inverse * inverse
             weight = weigh[k] * jnp.exp2(dist[k] * (narrow * -LOG2E))
@@ -213,13 +231,12 @@
             second_sum = jnp.sum(weight * dist[k], axis=0, keepdims=True)
             miss = jnp.log(count) - log_target
             move = jnp.clip(-miss * count / jnp.maximum(2.0 * second_sum * narrow, count), -0.5, 0.5)
-            length = length * jnp.exp(move)
             inverse = inverse * jnp.exp(-move)
         narrow = inverse * inverse
         weight = weigh[k] * jnp.exp2(dist[k] * (narrow * -LOG2E))
         count = own_mass + jnp.sum(weight, axis=0, keepdims=True)
-        length_ref[k : k + 1, :] = length
-        density_ref[k : k + 1, :] = count * (NORM * narrow * inverse)
+        inverse_ref[k : k + 1, :] = inverse
+        count_ref[k : k + 1, :] = count
 
     for trade in trades:
         trade.wait_send()
@@ -241,7 +258,7 @@
         any_space = pl.BlockSpec(memory_space=pl.ANY)
         vmem = pl.BlockSpec(memory_space=pltpu.VMEM)
         f32, i32 = jnp.float32, jnp.int32
-        length, density = pl.pallas_call(
+        inverse, count = pl.pallas_call(
             lambda *refs: kernel(n_grp, n_bis, knb, *refs),
             name="settle",
             out_shape=[jax.ShapeDtypeStruct((2, BLOCK), f32)] * 2,
@@ -267,17 +284,24 @@
                 pltpu.SemaphoreType.DMA,
                 pltpu.SemaphoreType.DMA,
                 pltpu.SemaphoreType.DMA,
+                pltpu.SemaphoreType.REGULAR((2,)),
             ],
             compiler_params=pltpu.CompilerParams(collective_id=0, has_side_effects=True, vmem_limit_bytes=4 << 20),
         )(
-            positions,
-            masses.reshape(2, BLOCK),
-            smoothing.reshape(2, BLOCK),
-            swap_lists.reshape(2),
-            send_lists.reshape(n_grp),
-            send_counts.reshape(n_grp),
-            neighbours,
+            *(
+                pltpu.with_memory_space_constraint(operand, pltpu.HBM)
+                for operand in (
+                    positions,
+                    masses.reshape(2, BLOCK),
+                    smoothing.reshape(2, BLOCK),
+                    swap_lists.reshape(2),
+                    send_lists.reshape(n_grp),
+                    send_counts.reshape(n_grp),
+                    neighbours,
+                )
+            )
         )
+        length, density = 1.0 / inverse, count * (NORM * inverse * inverse * inverse)
         return length.reshape(-1), density.reshape(-1)
 
     ranks = P(("grp", "bis"))

time: 24.6 us -> 21.4 us (0.87)
  local copies, waits for them, and re-layouts: 2.66 us -> 0 us
  Pallas kernels: 21 us -> 20.1 us
  other arithmetic: 0 us -> 0.57 us
    unnamed x16 -> x0, local copies, waits for them, and re-layouts: 2.66 us -> none
    pallas_call x1, Pallas kernels: 21 us -> 20.1 us  [on_device(): pl.pallas_call(lambda *refs: kernel(n_grp, n_bis, knb, *refs), name='sett...]
    reshape x0 -> x1, other arithmetic: none -> 0.57 us  [on_device(): return (length.reshape(-1), density.reshape(-1))]
where the time goes in v2:
time: 21.4 us; the launch traced here: 21.3 us
  Pallas kernels  20.1 us (94%)
  between operations  0.64 us (3%)
  other arithmetic  0.57 us (3%)
    pallas_call x1, Pallas kernels, on_device(): pl.pallas_call(lambda *refs: kernel(n_grp, n_bis, knb, *refs), name='sett...  20.1 us
    reshape x1, other arithmetic, on_device(): return (length.reshape(-1), density.reshape(-1))  0.57 us

profile of v2, /device:TPU:1, one launch (start us, length us, event | category | flops | bytes accessed | tf_op | source)
XLA Modules:
  0.0 21.3 jit_solution(2973952495253159000)
XLA Ops:
  0.6 20.1 %settle.1 = (f32[2,128]{1,0:T(2,128)S(1)}, f32[2,128]{1,0:T(2,128)S(1)}) custom-call(f32[3,256]{1,0:T(4,128)} %refs_0_.1, f32[2,128]{1,0:T(2,128)} %bitcast.9, f32[2,128]{1,0:T(2,128)} %bitcast.10, s32[2]{0:T(128)} %bitcast.11, s32[16]{0:T(128)} %bitcast.12, s32[16]{0:T(128)} %bitcast.13, s32[2,64,128]{2,1,0:T(8,128)} %refs_6_.1), custom_call_target="tpu_custom_call" | custom-call | tf_op jit(solution)/shard_map/settle/pallas_call | solution.py:261
  20.7 0.6 %fusion.1 = (f32[256]{0:T(256)}, f32[256]{0:T(256)}) fusion(f32[2,128]{1,0:T(2,128)S(1)} %get-tuple-element.5, f32[2,128]{1,0:T(2,128)S(1)} %get-tuple-element.4), kind=kLoop, calls=%fused_computation.2 | loop fusion | flops 1280 | bytes 4096 | tf_op jit(solution)/shard_map/reshape | solution.py:305

commit v3 on v2

--- a/solution.py
+++ b/solution.py
@@ -19,6 +19,10 @@
 
 def pick_rows(table, index):
     return jnp.take_along_axis(table, index, axis=0, mode="promise_in_bounds")
+
+
+def row_order(row):
+    return row // 2 * 2 + (row + row // 2) % 2
 
 
 def pick_lanes(table, index):
@@ -57,7 +61,8 @@
     trade_recv,
     deliver_send,
     deliver_recv,
-    beyond,
+    trade_here,
+    deliver_here,
 ):
     g = lax.axis_index("grp")
     b = lax.axis_index("bis")
@@ -69,38 +74,67 @@
     chips = n_grp // 2
     chip, core = g // 2, g % 2
 
-    def place(chip_step, core_step):
-        return (chip + chip_step) % chips * 2 + (core + core_step) % 2
-
-    order = sorted(
-        [(step, turn) for step in range(chips) for turn in range(2) if step or turn],
-        key=lambda hop: -min(hop[0], chips - hop[0]),
-    )
-
-    barrier = pltpu.get_barrier_semaphore()
-    for partner in (first, second, both):
-        pl.semaphore_signal(barrier, inc=1, device_id={"bis": partner}, device_id_type=MESH)
-    near_hops = [hop for hop in order if min(hop[0], chips - hop[0]) <= 2]
-    for hop in near_hops:
-        pl.semaphore_signal(barrier, inc=1, device_id={"grp": place(*hop)}, device_id_type=MESH)
-
     loads = [
         pltpu.make_async_copy(src, dst, load_sem.at[i])
         for i, (src, dst) in enumerate(
             [
-                (near_hbm, near),
                 (swap_hbm, swap),
                 (pos_hbm, pos),
                 (mass_hbm, mass),
                 (smooth_hbm, smooth),
                 (list_hbm, lists),
                 (count_hbm, counts),
+                (near_hbm, near),
             ]
         )
     ]
     for load in loads:
         load.start()
-    for load in loads[1:]:
+
+    trade_with = (first, second, both)
+    row = b // quarter
+    row_turn = row_order(row)
+    row_turns = [row_order(partner // quarter) for partner in trade_with]
+    corner = jnp.where(b == 0, 1, 0)
+    edge = n_grp // 2
+    turn = 2 * chip + 1 - core + jnp.where(g == 0, 15 * corner, 0)
+    turns = [1 + 15 * corner if to == 0 else to // 2 * 2 + 1 - to % 2 for to in range(n_grp)]
+    early_turns = jnp.where(turn < edge, turn - jnp.where(turn > 1, corner, 0), edge - corner)
+    by_turn = [to ^ 1 for to in range(n_grp)]
+
+    def ahead(other):
+        return (other < edge) & (other < turn)
+
+    barrier = pltpu.get_barrier_semaphore()
+    for partner, other in zip(trade_with, row_turns):
+
+        @pl.when(other > row_turn)
+        def _():
+            pl.semaphore_signal(barrier, inc=1, device_id={"bis": partner}, device_id_type=MESH)
+
+    for to in by_turn:
+
+        @pl.when((turn < edge) & (turns[to] > turn))
+        def _():
+            pl.semaphore_signal(barrier, inc=1, device_id={"grp": to}, device_id_type=MESH)
+
+    @pl.when(early_turns + row_turn > 0)
+    def _():
+        pl.semaphore_wait(barrier, early_turns + row_turn)
+
+    for i, (partner, other) in enumerate(zip(trade_with, row_turns)):
+
+        @pl.when(other < row_turn)
+        def _():
+            pl.semaphore_signal(trade_here.at[i], inc=1, device_id={"bis": partner}, device_id_type=MESH)
+
+    for to in by_turn:
+
+        @pl.when(ahead(turns[to]))
+        def _():
+            pl.semaphore_signal(deliver_here, inc=1, device_id={"grp": to}, device_id_type=MESH)
+
+    for load in loads[:-1]:
         load.wait()
 
     l0, l1 = swap[0], swap[1]
@@ -113,10 +147,6 @@
     whole = lambda value: jnp.full((ROWS, BLOCK), value, jnp.int32)
     trade_out[0] = jnp.where(whole(l0) == 0, blocks[0], blocks[1])
     trade_out[1] = jnp.where(whole(l1) == 0, blocks[0], blocks[1])
-
-    pl.semaphore_wait(barrier, len(near_hops) + 3)
-    for side, step in enumerate((2, chips - 2)):
-        pl.semaphore_signal(beyond.at[side], inc=1, device_id={"grp": place(step, 0)}, device_id_type=MESH)
 
     trades = [
         pltpu.make_async_remote_copy(
@@ -129,10 +159,16 @@
         )
         for src, dst, partner in ((0, 0, first), (1, 1, second), (0, 2, both))
     ]
-    for trade in trades:
-        trade.start()
-
-    loads[0].wait()
+    for trade, other in zip(trades, row_turns):
+        pl.when(other < row_turn)(trade.start)
+    for i in (1, 2, 0):
+
+        @pl.when(row_turns[i] > row_turn)
+        def _():
+            pl.semaphore_wait(trade_here.at[i], 1)
+            trades[i].start()
+
+    loads[-1].wait()
     for k in range(2):
         slot = near[k]
         turned = pltpu.roll(slot, 1, 1, stride=1, stride_axis=0)
@@ -157,25 +193,35 @@
         blocks[k] = jnp.where(whole(l1) == k, from_second, block)
         final[k] = blocks[k]
 
-    for side in range(2):
-        pl.semaphore_wait(beyond.at[side], 1)
-    for hop in [*order, (0, 0)]:
-        to = place(*hop)
-        slot = pl.ds(SENT * (2 * hop[0] + hop[1]), SENT)
+    delivers = []
+    for to in by_turn:
         block = jnp.where(whole(lists[to]) == 0, blocks[0], blocks[1])
         block = jnp.where(whole(counts[to]) > 0, block, 0.0)
-        if hop == (0, 0):
-            deliver_in[slot] = block[0:SENT]
-            continue
-        deliver_out[slot] = block[0:SENT]
-        pltpu.make_async_remote_copy(
-            src_ref=deliver_out.at[slot],
-            dst_ref=deliver_in.at[slot],
+        offset = (to // 2 - chip + chips) % chips * 2 + (to + core) % 2
+        deliver_out[to, 0:SENT] = block[0:SENT]
+        deliver = pltpu.make_async_remote_copy(
+            src_ref=deliver_out.at[to, pl.ds(0, SENT)],
+            dst_ref=deliver_in.at[offset, pl.ds(0, SENT)],
             send_sem=deliver_send,
             recv_sem=deliver_recv,
             device_id={"grp": to},
             device_id_type=MESH,
-        ).start()
+        )
+        pl.when(ahead(turns[to]))(deliver.start)
+        delivers.append((to, deliver))
+
+    block = jnp.where(whole(lists[g]) == 0, blocks[0], blocks[1])
+    deliver_in[0] = jnp.where(whole(counts[g]) > 0, block, 0.0)
+
+    pl.semaphore_wait(deliver_here, jnp.where(turn < edge, n_grp - 1 - early_turns, 1))
+    for to in range(n_grp):
+
+        @pl.when((chip == chips // 2 - 1) & (core == to % 2) & (turns[to] >= edge))
+        def _():
+            pl.semaphore_signal(deliver_here, inc=1, device_id={"grp": to}, device_id_type=MESH)
+
+    for to, deliver in delivers:
+        pl.when(jnp.logical_not(ahead(turns[to])) & (g != to))(deliver.start)
 
     own_rows = [jnp.concatenate([blocks[k][c : c + 1] for k in (0, 1) for _ in range(4)], axis=0) for c in range(4)]
     for k in range(2):
@@ -184,16 +230,17 @@
             moved[k, c] = pltpu.roll(row, 1, 1, stride=1, stride_axis=0)
 
     pltpu.make_async_remote_copy(
-        src_ref=deliver_in.at[pl.ds(SENT, SENT * (n_grp - 1))],
-        dst_ref=deliver_in.at[pl.ds(SENT, SENT * (n_grp - 1))],
+        src_ref=deliver_in.at[pl.ds(1, n_grp - 1), pl.ds(0, SENT)],
+        dst_ref=deliver_in.at[pl.ds(1, n_grp - 1), pl.ds(0, SENT)],
         send_sem=deliver_send,
         recv_sem=deliver_recv,
         device_id={"grp": g},
         device_id_type=MESH,
     ).wait_recv()
 
-    low = [deliver_in[pl.ds(c, 8, stride=SENT), :] for c in range(4)]
-    high = [deliver_in[pl.ds(8 * SENT + c, 8, stride=SENT), :] for c in range(4)]
+    flat = deliver_in.reshape(n_grp * ROWS, BLOCK)
+    low = [flat[pl.ds(c, 8, stride=ROWS), :] for c in range(4)]
+    high = [flat[pl.ds(8 * ROWS + c, 8, stride=ROWS), :] for c in range(4)]
     lane = lax.broadcasted_iota(jnp.int32, (8, BLOCK), 1)
     row = lax.broadcasted_iota(jnp.int32, (8, BLOCK), 0)
     dist, weigh = [], []
@@ -241,8 +288,8 @@
     for trade in trades:
         trade.wait_send()
     pltpu.make_async_remote_copy(
-        src_ref=deliver_out.at[pl.ds(SENT, SENT * (n_grp - 1))],
-        dst_ref=deliver_out.at[pl.ds(SENT, SENT * (n_grp - 1))],
+        src_ref=deliver_out.at[pl.ds(1, n_grp - 1), pl.ds(0, SENT)],
+        dst_ref=deliver_out.at[pl.ds(1, n_grp - 1), pl.ds(0, SENT)],
         send_sem=deliver_send,
         recv_sem=deliver_recv,
         device_id={"grp": g},
@@ -276,15 +323,16 @@
                 pltpu.VMEM((2, ROWS, BLOCK), f32),
                 pltpu.VMEM((3, ROWS, BLOCK), f32),
                 pltpu.VMEM((2, ROWS, BLOCK), f32),
-                pltpu.VMEM((SENT * n_grp, BLOCK), f32),
-                pltpu.VMEM((SENT * n_grp, BLOCK), f32),
+                pltpu.VMEM((n_grp, ROWS, BLOCK), f32),
+                pltpu.VMEM((n_grp, ROWS, BLOCK), f32),
                 pltpu.VMEM((2, 3, knb, BLOCK), f32),
                 pltpu.SemaphoreType.DMA((7,)),
                 pltpu.SemaphoreType.DMA,
                 pltpu.SemaphoreType.DMA,
                 pltpu.SemaphoreType.DMA,
                 pltpu.SemaphoreType.DMA,
-                pltpu.SemaphoreType.REGULAR((2,)),
+                pltpu.SemaphoreType.REGULAR((3,)),
+                pltpu.SemaphoreType.REGULAR,
             ],
             compiler_params=pltpu.CompilerParams(collective_id=0, has_side_effects=True, vmem_limit_bytes=4 << 20),
         )(

time: 21.4 us -> 20.3 us (0.949)
  Pallas kernels: 20.1 us -> 19 us
    pallas_call x1, Pallas kernels: 20.1 us -> 19 us  [on_device(): pl.pallas_call(lambda *refs: kernel(n_grp, n_bis, knb, *refs), name='sett...]
where the time goes in v3:
time: 20.3 us; the launch traced here: 20.2 us
  Pallas kernels  19 us (94%)
  between operations  0.64 us (3%)
  other arithmetic  0.57 us (3%)
    pallas_call x1, Pallas kernels, on_device(): pl.pallas_call(lambda *refs: kernel(n_grp, n_bis, knb, *refs), name='sett...  19 us
    reshape x1, other arithmetic, on_device(): return (length.reshape(-1), density.reshape(-1))  0.57 us

profile of v3, /device:TPU:1, one launch (start us, length us, event | category | flops | bytes accessed | tf_op | source)
XLA Modules:
  0.0 20.2 jit_solution(11066639680300749188)
XLA Ops:
  0.6 19.0 %settle.1 = (f32[2,128]{1,0:T(2,128)S(1)}, f32[2,128]{1,0:T(2,128)S(1)}) custom-call(f32[3,256]{1,0:T(4,128)} %refs_0_.1, f32[2,128]{1,0:T(2,128)} %bitcast.9, f32[2,128]{1,0:T(2,128)} %bitcast.10, s32[2]{0:T(128)} %bitcast.11, s32[16]{0:T(128)} %bitcast.12, s32[16]{0:T(128)} %bitcast.13, s32[2,64,128]{2,1,0:T(8,128)} %refs_6_.1), custom_call_target="tpu_custom_call" | custom-call | tf_op jit(solution)/shard_map/settle/pallas_call | solution.py:308
  19.6 0.6 %fusion.1 = (f32[256]{0:T(256)}, f32[256]{0:T(256)}) fusion(f32[2,128]{1,0:T(2,128)S(1)} %get-tuple-element.5, f32[2,128]{1,0:T(2,128)S(1)} %get-tuple-element.4), kind=kLoop, calls=%fused_computation.2 | loop fusion | flops 1280 | bytes 4096 | tf_op jit(solution)/shard_map/reshape | solution.py:353

commit v4 on v3

--- a/solution.py
+++ b/solution.py
@@ -55,12 +55,16 @@
     final,
     deliver_out,
     deliver_in,
+    raw_out,
+    direct_in,
     moved,
     load_sem,
     trade_send,
     trade_recv,
     deliver_send,
     deliver_recv,
+    direct_send,
+    direct_recv,
     trade_here,
     deliver_here,
 ):
@@ -102,6 +106,15 @@
     early_turns = jnp.where(turn < edge, turn - jnp.where(turn > 1, corner, 0), edge - corner)
     by_turn = [to ^ 1 for to in range(n_grp)]
 
+    late = chip >= chips // 2
+    front = (chip == 0) & (turn < edge)
+    late_devices = range(n_grp // 2, n_grp)
+    fronts = 6 - sum(jnp.where(partner == 0, 1, 0) for partner in trade_with)
+    announced = early_turns + row_turn + jnp.where(late, fronts, 0)
+
+    def to_front(partner, to):
+        return late & (partner + to > 0)
+
     def ahead(other):
         return (other < edge) & (other < turn)
 
@@ -118,9 +131,15 @@
         def _():
             pl.semaphore_signal(barrier, inc=1, device_id={"grp": to}, device_id_type=MESH)
 
-    @pl.when(early_turns + row_turn > 0)
+    @pl.when(front)
     def _():
-        pl.semaphore_wait(barrier, early_turns + row_turn)
+        for partner in trade_with:
+            for to in late_devices:
+                pl.semaphore_signal(barrier, inc=1, device_id={"bis": partner, "grp": to}, device_id_type=MESH)
+
+    @pl.when(announced > 0)
+    def _():
+        pl.semaphore_wait(barrier, announced)
 
     for i, (partner, other) in enumerate(zip(trade_with, row_turns)):
 
@@ -161,6 +180,36 @@
     ]
     for trade, other in zip(trades, row_turns):
         pl.when(other < row_turn)(trade.start)
+    place = (chip - chips // 2) * 2 + core
+    directs = []
+    for to in (1, 0):
+        for src, kind, partner in ((0, 1, first), (1, 2, second), (0, 3, both)):
+            direct = pltpu.make_async_remote_copy(
+                src_ref=trade_out.at[src],
+                dst_ref=direct_in.at[place, kind],
+                send_sem=direct_send,
+                recv_sem=direct_recv,
+                device_id={"bis": partner, "grp": to},
+                device_id_type=MESH,
+            )
+            pl.when(to_front(partner, to))(direct.start)
+            directs.append((direct, to_front(partner, to)))
+    rows = lax.broadcasted_iota(jnp.int32, (ROWS, BLOCK), 0)
+    for to in (1, 0):
+        chosen = whole(lists[to])
+        code = jnp.where(chosen == l1, 3.0, jnp.where(chosen == l0, 2.0, 1.0))
+        code = jnp.where(whole(counts[to]) > 0, code, 0.0)
+        raw_out[to] = jnp.where(rows == SENT, code, jnp.where(chosen == 0, blocks[0], blocks[1]))
+        direct = pltpu.make_async_remote_copy(
+            src_ref=raw_out.at[to],
+            dst_ref=direct_in.at[place, 0],
+            send_sem=direct_send,
+            recv_sem=direct_recv,
+            device_id={"grp": to},
+            device_id_type=MESH,
+        )
+        pl.when(to_front(b, to))(direct.start)
+        directs.append((direct, to_front(b, to)))
     for i in (1, 2, 0):
 
         @pl.when(row_turns[i] > row_turn)
@@ -207,7 +256,10 @@
             device_id={"grp": to},
             device_id_type=MESH,
         )
-        pl.when(ahead(turns[to]))(deliver.start)
+        sends = ahead(turns[to])
+        if to < 2:
+            sends = sends & jnp.logical_not(late)
+        pl.when(sends)(deliver.start)
         delivers.append((to, deliver))
 
     block = jnp.where(whole(lists[g]) == 0, blocks[0], blocks[1])
@@ -229,14 +281,38 @@
             row = jnp.broadcast_to(blocks[k][c : c + 1], (knb, BLOCK))
             moved[k, c] = pltpu.roll(row, 1, 1, stride=1, stride_axis=0)
 
-    pltpu.make_async_remote_copy(
-        src_ref=deliver_in.at[pl.ds(1, n_grp - 1), pl.ds(0, SENT)],
-        dst_ref=deliver_in.at[pl.ds(1, n_grp - 1), pl.ds(0, SENT)],
-        send_sem=deliver_send,
-        recv_sem=deliver_recv,
-        device_id={"grp": g},
-        device_id_type=MESH,
-    ).wait_recv()
+    def delivered(ref, number):
+        part = ref.at[pl.ds(1, number), pl.ds(0, SENT)]
+        return pltpu.make_async_remote_copy(
+            src_ref=part,
+            dst_ref=part,
+            send_sem=deliver_send,
+            recv_sem=deliver_recv,
+            device_id={"grp": g},
+            device_id_type=MESH,
+        )
+
+    pl.when(jnp.logical_not(front))(delivered(deliver_in, n_grp - 1).wait_recv)
+
+    @pl.when(front)
+    def _():
+        delivered(deliver_in, n_grp // 2 - 1).wait_recv()
+        pltpu.make_async_remote_copy(
+            src_ref=direct_in,
+            dst_ref=direct_in,
+            send_sem=direct_send,
+            recv_sem=direct_recv,
+            device_id={"grp": g},
+            device_id_type=MESH,
+        ).wait_recv()
+        for source in range(n_grp // 2):
+            raw, one, two, three = (direct_in[source, kind] for kind in range(4))
+            code = jnp.broadcast_to(raw[SENT : SENT + 1], (ROWS, BLOCK))
+            kept = jnp.broadcast_to(two[5:6], (ROWS, BLOCK)) != 0.0
+            block = jnp.where(code == 3.0, jnp.where(kept, two, three), jnp.where(code == 2.0, one, raw))
+            block = jnp.where(code == 0.0, 0.0, block)
+            offset = 2 * (chips // 2 - source // 2) + (core + source) % 2
+            deliver_in[offset, 0:SENT] = block[0:SENT]
 
     flat = deliver_in.reshape(n_grp * ROWS, BLOCK)
     low = [flat[pl.ds(c, 8, stride=ROWS), :] for c in range(4)]
@@ -287,14 +363,11 @@
 
     for trade in trades:
         trade.wait_send()
-    pltpu.make_async_remote_copy(
-        src_ref=deliver_out.at[pl.ds(1, n_grp - 1), pl.ds(0, SENT)],
-        dst_ref=deliver_out.at[pl.ds(1, n_grp - 1), pl.ds(0, SENT)],
-        send_sem=deliver_send,
-        recv_sem=deliver_recv,
-        device_id={"grp": g},
-        device_id_type=MESH,
-    ).wait_send()
+    for direct, sent in directs:
+        pl.when(sent)(direct.wait_send)
+    pl.when(jnp.logical_not(late))(delivered(deliver_out, n_grp - 1).wait_send)
+    pl.when(late)(delivered(deliver_out, n_grp - 3).wait_send)
+    pl.when(late & (b == 0))(delivered(deliver_out, 1).wait_send)
 
 
 def solution(mesh):
@@ -325,8 +398,12 @@
                 pltpu.VMEM((2, ROWS, BLOCK), f32),
                 pltpu.VMEM((n_grp, ROWS, BLOCK), f32),
                 pltpu.VMEM((n_grp, ROWS, BLOCK), f32),
+                pltpu.VMEM((2, ROWS, BLOCK), f32),
+                pltpu.VMEM((n_grp // 2, 4, ROWS, BLOCK), f32),
                 pltpu.VMEM((2, 3, knb, BLOCK), f32),
                 pltpu.SemaphoreType.DMA((7,)),
+                pltpu.SemaphoreType.DMA,
+                pltpu.SemaphoreType.DMA,
                 pltpu.SemaphoreType.DMA,
                 pltpu.SemaphoreType.DMA,
                 pltpu.SemaphoreType.DMA,

time: 20.3 us -> 19.2 us (0.946)
  the two profiles are of different devices: /device:TPU:1 before, /device:TPU:111 now
where the time goes in v4:
time: 19.2 us; the launch traced here: 19 us
  Pallas kernels  17.8 us (93%)
  between operations  0.64 us (3%)
  other arithmetic  0.57 us (3%)
    pallas_call x1, Pallas kernels, on_device(): pl.pallas_call(lambda *refs: kernel(n_grp, n_bis, knb, *refs), name='sett...  17.8 us
    reshape x1, other arithmetic, on_device(): return (length.reshape(-1), density.reshape(-1))  0.57 us

profile of v4, /device:TPU:111, one launch (start us, length us, event | category | flops | bytes accessed | tf_op | source)
XLA Modules:
  0.0 19.0 jit_solution(13409208667434794318)
XLA Ops:
  0.6 17.8 %settle.1 = (f32[2,128]{1,0:T(2,128)S(1)}, f32[2,128]{1,0:T(2,128)S(1)}) custom-call(f32[3,256]{1,0:T(4,128)} %refs_0_.1, f32[2,128]{1,0:T(2,128)} %bitcast.9, f32[2,128]{1,0:T(2,128)} %bitcast.10, s32[2]{0:T(128)} %bitcast.11, s32[16]{0:T(128)} %bitcast.12, s32[16]{0:T(128)} %bitcast.13, s32[2,64,128]{2,1,0:T(8,128)} %refs_6_.1), custom_call_target="tpu_custom_call" | custom-call | tf_op jit(solution)/shard_map/settle/pallas_call | solution.py:381
  18.5 0.6 %fusion.1 = (f32[256]{0:T(256)}, f32[256]{0:T(256)}) fusion(f32[2,128]{1,0:T(2,128)S(1)} %get-tuple-element.5, f32[2,128]{1,0:T(2,128)S(1)} %get-tuple-element.4), kind=kLoop, calls=%fused_computation.2 | loop fusion | flops 1280 | bytes 4096 | tf_op jit(solution)/shard_map/reshape | solution.py:430

commit v5 on v4

--- a/solution.py
+++ b/solution.py
@@ -10,6 +10,7 @@
 BLOCK = 128
 ROWS = 8
 SENT = 4
+FRONT = 2
 ITERS = 3
 TARGET = 16.0
 NORM = math.pi**-1.5
@@ -55,7 +56,7 @@
     final,
     deliver_out,
     deliver_in,
-    raw_out,
+    direct_out,
     direct_in,
     moved,
     load_sem,
@@ -107,9 +108,10 @@
     by_turn = [to ^ 1 for to in range(n_grp)]
 
     late = chip >= chips // 2
-    front = (chip == 0) & (turn < edge)
+    front = (chip < FRONT) & (turn < edge)
     late_devices = range(n_grp // 2, n_grp)
-    fronts = 6 - sum(jnp.where(partner == 0, 1, 0) for partner in trade_with)
+    front_devices = [to ^ 1 for to in range(2 * FRONT)]
+    fronts = 6 * FRONT - sum(jnp.where(partner == 0, 1, 0) for partner in trade_with)
     announced = early_turns + row_turn + jnp.where(late, fronts, 0)
 
     def to_front(partner, to):
@@ -169,8 +171,8 @@
 
     trades = [
         pltpu.make_async_remote_copy(
-            src_ref=trade_out.at[src],
-            dst_ref=trade_in.at[dst],
+            src_ref=trade_out.at[src, pl.ds(0, 6)],
+            dst_ref=trade_in.at[dst, pl.ds(0, 6)],
             send_sem=trade_send,
             recv_sem=trade_recv,
             device_id={"bis": partner},
@@ -181,35 +183,32 @@
     for trade, other in zip(trades, row_turns):
         pl.when(other < row_turn)(trade.start)
     place = (chip - chips // 2) * 2 + core
+    rows = lax.broadcasted_iota(jnp.int32, (ROWS, BLOCK), 0)
+    direct_out[2 * FRONT] = jnp.where(rows == SENT, jnp.broadcast_to(flag, (ROWS, BLOCK)), trade_out[1])
+    for to in front_devices:
+        chosen = whole(lists[to])
+        code = jnp.where(chosen == l1, 3.0, jnp.where(chosen == l0, 2.0, 1.0))
+        code = jnp.where(whole(counts[to]) > 0, code, 0.0)
+        direct_out[to] = jnp.where(rows == SENT, code, jnp.where(chosen == 0, blocks[0], blocks[1]))
     directs = []
-    for to in (1, 0):
-        for src, kind, partner in ((0, 1, first), (1, 2, second), (0, 3, both)):
+    for to in front_devices:
+        for src, kind, height, partner in (
+            (trade_out.at[0], 1, SENT, first),
+            (direct_out.at[2 * FRONT], 2, SENT + 1, second),
+            (trade_out.at[0], 3, SENT, both),
+            (direct_out.at[to], 0, SENT + 1, b),
+        ):
             direct = pltpu.make_async_remote_copy(
-                src_ref=trade_out.at[src],
-                dst_ref=direct_in.at[place, kind],
+                src_ref=src.at[pl.ds(0, height)],
+                dst_ref=direct_in.at[place, kind, pl.ds(0, height)],
                 send_sem=direct_send,
                 recv_sem=direct_recv,
                 device_id={"bis": partner, "grp": to},
                 device_id_type=MESH,
             )
-            pl.when(to_front(partner, to))(direct.start)
-            directs.append((direct, to_front(partner, to)))
-    rows = lax.broadcasted_iota(jnp.int32, (ROWS, BLOCK), 0)
-    for to in (1, 0):
-        chosen = whole(lists[to])
-        code = jnp.where(chosen == l1, 3.0, jnp.where(chosen == l0, 2.0, 1.0))
-        code = jnp.where(whole(counts[to]) > 0, code, 0.0)
-        raw_out[to] = jnp.where(rows == SENT, code, jnp.where(chosen == 0, blocks[0], blocks[1]))
-        direct = pltpu.make_async_remote_copy(
-            src_ref=raw_out.at[to],
-            dst_ref=direct_in.at[place, 0],
-            send_sem=direct_send,
-            recv_sem=direct_recv,
-            device_id={"grp": to},
-            device_id_type=MESH,
-        )
-        pl.when(to_front(b, to))(direct.start)
-        directs.append((direct, to_front(b, to)))
+            sent = to_front(partner, to)
+            pl.when(sent)(direct.start)
+            directs.append((direct, sent))
     for i in (1, 2, 0):
 
         @pl.when(row_turns[i] > row_turn)
@@ -226,8 +225,8 @@
         index[k] = jnp.where(turned < 2, turned, 2 + offset)
 
     pltpu.make_async_remote_copy(
-        src_ref=trade_in,
-        dst_ref=trade_in,
+        src_ref=trade_in.at[:, pl.ds(0, 6)],
+        dst_ref=trade_in.at[:, pl.ds(0, 6)],
         send_sem=trade_send,
         recv_sem=trade_recv,
         device_id={"bis": first},
@@ -257,7 +256,7 @@
             device_id_type=MESH,
         )
         sends = ahead(turns[to])
-        if to < 2:
+        if to < 2 * FRONT:
             sends = sends & jnp.logical_not(late)
         pl.when(sends)(deliver.start)
         delivers.append((to, deliver))
@@ -297,9 +296,10 @@
     @pl.when(front)
     def _():
         delivered(deliver_in, n_grp // 2 - 1).wait_recv()
+        part = direct_in.reshape(n_grp // 2 * 4 * ROWS, BLOCK).at[pl.ds(0, n_grp // 2 * (4 * SENT + 2))]
         pltpu.make_async_remote_copy(
-            src_ref=direct_in,
-            dst_ref=direct_in,
+            src_ref=part,
+            dst_ref=part,
             send_sem=direct_send,
             recv_sem=direct_recv,
             device_id={"grp": g},
@@ -308,10 +308,10 @@
         for source in range(n_grp // 2):
             raw, one, two, three = (direct_in[source, kind] for kind in range(4))
             code = jnp.broadcast_to(raw[SENT : SENT + 1], (ROWS, BLOCK))
-            kept = jnp.broadcast_to(two[5:6], (ROWS, BLOCK)) != 0.0
+            kept = jnp.broadcast_to(two[SENT : SENT + 1], (ROWS, BLOCK)) != 0.0
             block = jnp.where(code == 3.0, jnp.where(kept, two, three), jnp.where(code == 2.0, one, raw))
             block = jnp.where(code == 0.0, 0.0, block)
-            offset = 2 * (chips // 2 - source // 2) + (core + source) % 2
+            offset = 2 * (chip + chips // 2 - source // 2) + (core + source) % 2
             deliver_in[offset, 0:SENT] = block[0:SENT]
 
     flat = deliver_in.reshape(n_grp * ROWS, BLOCK)
@@ -366,7 +366,7 @@
     for direct, sent in directs:
         pl.when(sent)(direct.wait_send)
     pl.when(jnp.logical_not(late))(delivered(deliver_out, n_grp - 1).wait_send)
-    pl.when(late)(delivered(deliver_out, n_grp - 3).wait_send)
+    pl.when(late)(delivered(deliver_out, n_grp - 1 - 2 * FRONT).wait_send)
     pl.when(late & (b == 0))(delivered(deliver_out, 1).wait_send)
 
 
@@ -398,7 +398,7 @@
                 pltpu.VMEM((2, ROWS, BLOCK), f32),
                 pltpu.VMEM((n_grp, ROWS, BLOCK), f32),
                 pltpu.VMEM((n_grp, ROWS, BLOCK), f32),
-                pltpu.VMEM((2, ROWS, BLOCK), f32),
+                pltpu.VMEM((2 * FRONT + 1, ROWS, BLOCK), f32),
                 pltpu.VMEM((n_grp // 2, 4, ROWS, BLOCK), f32),
                 pltpu.VMEM((2, 3, knb, BLOCK), f32),
                 pltpu.SemaphoreType.DMA((7,)),

time: 19.2 us -> 18.6 us (0.969)
  the two profiles are of different devices: /device:TPU:111 before, /device:TPU:1 now
where the time goes in v5:
time: 18.6 us; the launch traced here: 18.4 us
  Pallas kernels  17.2 us (92%)
  between operations  0.64 us (3%)
  other arithmetic  0.57 us (3%)
    pallas_call x1, Pallas kernels, on_device(): pl.pallas_call(lambda *refs: kernel(n_grp, n_bis, knb, *refs), name='sett...  17.2 us
    reshape x1, other arithmetic, on_device(): return (length.reshape(-1), density.reshape(-1))  0.57 us

profile of v5, /device:TPU:1, one launch (start us, length us, event | category | flops | bytes accessed | tf_op | source)
XLA Modules:
  0.0 18.4 jit_solution(772851927118234404)
XLA Ops:
  0.6 17.2 %settle.1 = (f32[2,128]{1,0:T(2,128)S(1)}, f32[2,128]{1,0:T(2,128)S(1)}) custom-call(f32[3,256]{1,0:T(4,128)} %refs_0_.1, f32[2,128]{1,0:T(2,128)} %bitcast.9, f32[2,128]{1,0:T(2,128)} %bitcast.10, s32[2]{0:T(128)} %bitcast.11, s32[16]{0:T(128)} %bitcast.12, s32[16]{0:T(128)} %bitcast.13, s32[2,64,128]{2,1,0:T(8,128)} %refs_6_.1), custom_call_target="tpu_custom_call" | custom-call | tf_op jit(solution)/shard_map/settle/pallas_call | solution.py:381
  17.9 0.6 %fusion.1 = (f32[256]{0:T(256)}, f32[256]{0:T(256)}) fusion(f32[2,128]{1,0:T(2,128)S(1)} %get-tuple-element.5, f32[2,128]{1,0:T(2,128)S(1)} %get-tuple-element.4), kind=kLoop, calls=%fused_computation.2 | loop fusion | flops 1280 | bytes 4096 | tf_op jit(solution)/shard_map/reshape | solution.py:430

commit v6 on v5

--- a/solution.py
+++ b/solution.py
@@ -206,9 +206,10 @@
                 device_id={"bis": partner, "grp": to},
                 device_id_type=MESH,
             )
-            sent = to_front(partner, to)
+            directs.append((to, direct, to_front(partner, to)))
+    for to, direct, sent in directs:
+        if to < 2:
             pl.when(sent)(direct.start)
-            directs.append((direct, sent))
     for i in (1, 2, 0):
 
         @pl.when(row_turns[i] > row_turn)
@@ -223,6 +224,10 @@
         source = turned - 2
         offset = ((2 * chip - (source & -2)) & (n_grp - 1)) + ((core - source) & 1)
         index[k] = jnp.where(turned < 2, turned, 2 + offset)
+
+    for to, direct, sent in directs:
+        if to >= 2:
+            pl.when(sent)(direct.start)
 
     pltpu.make_async_remote_copy(
         src_ref=trade_in.at[:, pl.ds(0, 6)],
@@ -291,20 +296,36 @@
             device_id_type=MESH,
         )
 
-    pl.when(jnp.logical_not(front))(delivered(deliver_in, n_grp - 1).wait_recv)
-
-    @pl.when(front)
-    def _():
-        delivered(deliver_in, n_grp // 2 - 1).wait_recv()
-        part = direct_in.reshape(n_grp // 2 * 4 * ROWS, BLOCK).at[pl.ds(0, n_grp // 2 * (4 * SENT + 2))]
-        pltpu.make_async_remote_copy(
+    for trade in trades:
+        trade.wait_send()
+    flat_direct = direct_in.reshape(n_grp // 2 * 4 * ROWS, BLOCK)
+
+    def directed(height):
+        part = flat_direct.at[pl.ds(0, height)]
+        return pltpu.make_async_remote_copy(
             src_ref=part,
             dst_ref=part,
             send_sem=direct_send,
             recv_sem=direct_recv,
             device_id={"grp": g},
             device_id_type=MESH,
-        ).wait_recv()
+        )
+
+    heights = 2 * FRONT * (4 * SENT + 2)
+    low_skip = (b == 0) | (second == 0)
+    high_skip = (first == 0) | (both == 0)
+    pl.when(late & jnp.logical_not(low_skip | high_skip))(directed(heights).wait_send)
+    pl.when(late & low_skip)(directed(heights - SENT - 1).wait_send)
+    pl.when(late & high_skip)(directed(heights - SENT).wait_send)
+    pl.when(jnp.logical_not(late))(delivered(deliver_out, n_grp - 1).wait_send)
+    pl.when(late)(delivered(deliver_out, n_grp - 1 - 2 * FRONT).wait_send)
+    pl.when(late & (b == 0))(delivered(deliver_out, 1).wait_send)
+    pl.when(jnp.logical_not(front))(delivered(deliver_in, n_grp - 1).wait_recv)
+
+    @pl.when(front)
+    def _():
+        delivered(deliver_in, n_grp // 2 - 1).wait_recv()
+        directed(n_grp // 2 * (4 * SENT + 2)).wait_recv()
         for source in range(n_grp // 2):
             raw, one, two, three = (direct_in[source, kind] for kind in range(4))
             code = jnp.broadcast_to(raw[SENT : SENT + 1], (ROWS, BLOCK))
@@ -360,14 +381,6 @@
         count = own_mass + jnp.sum(weight, axis=0, keepdims=True)
         inverse_ref[k : k + 1, :] = inverse
         count_ref[k : k + 1, :] = count
-
-    for trade in trades:
-        trade.wait_send()
-    for direct, sent in directs:
-        pl.when(sent)(direct.wait_send)
-    pl.when(jnp.logical_not(late))(delivered(deliver_out, n_grp - 1).wait_send)
-    pl.when(late)(delivered(deliver_out, n_grp - 1 - 2 * FRONT).wait_send)
-    pl.when(late & (b == 0))(delivered(deliver_out, 1).wait_send)
 
 
 def solution(mesh):

time: 18.6 us -> 18.5 us (level)
  no operation moved by 1% of the time
where the time goes in v6:
time: 18.5 us; the launch traced here: 18.4 us
  Pallas kernels  17.2 us (93%)
  between operations  0.64 us (3%)
  other arithmetic  0.57 us (3%)
    pallas_call x1, Pallas kernels, on_device(): pl.pallas_call(lambda *refs: kernel(n_grp, n_bis, knb, *refs), name='sett...  17.2 us
    reshape x1, other arithmetic, on_device(): return (length.reshape(-1), density.reshape(-1))  0.57 us

profile of v6, /device:TPU:1, one launch (start us, length us, event | category | flops | bytes accessed | tf_op | source)
XLA Modules:
  0.0 18.4 jit_solution(11749256097598321483)
XLA Ops:
  0.6 17.2 %settle.1 = (f32[2,128]{1,0:T(2,128)S(1)}, f32[2,128]{1,0:T(2,128)S(1)}) custom-call(f32[3,256]{1,0:T(4,128)} %refs_0_.1, f32[2,128]{1,0:T(2,128)} %bitcast.9, f32[2,128]{1,0:T(2,128)} %bitcast.10, s32[2]{0:T(128)} %bitcast.11, s32[16]{0:T(128)} %bitcast.12, s32[16]{0:T(128)} %bitcast.13, s32[2,64,128]{2,1,0:T(8,128)} %refs_6_.1), custom_call_target="tpu_custom_call" | custom-call | tf_op jit(solution)/shard_map/settle/pallas_call | solution.py:394
  17.8 0.6 %fusion.1 = (f32[256]{0:T(256)}, f32[256]{0:T(256)}) fusion(f32[2,128]{1,0:T(2,128)S(1)} %get-tuple-element.5, f32[2,128]{1,0:T(2,128)S(1)} %get-tuple-element.4), kind=kLoop, calls=%fused_computation.2 | loop fusion | flops 1280 | bytes 4096 | tf_op jit(solution)/shard_map/reshape | solution.py:443

commit v7 on v6

--- a/solution.py
+++ b/solution.py
@@ -10,7 +10,7 @@
 BLOCK = 128
 ROWS = 8
 SENT = 4
-FRONT = 2
+FRONT = 3
 ITERS = 3
 TARGET = 16.0
 NORM = math.pi**-1.5
@@ -18,16 +18,15 @@
 MESH = pl.DeviceIdType.MESH
 
 
-def pick_rows(table, index):
-    return jnp.take_along_axis(table, index, axis=0, mode="promise_in_bounds")
+def pick(table, index, axis):
+    other = (1 - axis,)
+    numbers = lax.GatherDimensionNumbers((), (axis,), (axis,), other, other)
+    mode = lax.GatherScatterMode.PROMISE_IN_BOUNDS
+    return lax.gather(table, index[..., None], numbers, (1, 1), mode=mode)
 
 
 def row_order(row):
     return row // 2 * 2 + (row + row // 2) % 2
-
-
-def pick_lanes(table, index):
-    return jnp.take_along_axis(table, index, axis=1, mode="promise_in_bounds")
 
 
 def kernel(
@@ -59,6 +58,7 @@
     direct_out,
     direct_in,
     moved,
+    picked,
     load_sem,
     trade_send,
     trade_recv,
@@ -108,14 +108,15 @@
     by_turn = [to ^ 1 for to in range(n_grp)]
 
     late = chip >= chips // 2
-    front = (chip < FRONT) & (turn < edge)
+    front = (turn < edge) & ((chip == 0) | ((chip < FRONT) & (row >= 2)))
     late_devices = range(n_grp // 2, n_grp)
     front_devices = [to ^ 1 for to in range(2 * FRONT)]
-    fronts = 6 * FRONT - sum(jnp.where(partner == 0, 1, 0) for partner in trade_with)
+    fronts = 6 - sum(jnp.where(partner == 0, 1, 0) for partner in trade_with)
+    fronts = fronts + 2 * (FRONT - 1) * jnp.where(row < 2, 2, 1)
     announced = early_turns + row_turn + jnp.where(late, fronts, 0)
 
     def to_front(partner, to):
-        return late & (partner + to > 0)
+        return late & ((partner + to > 0) if to < 2 else (partner >= half))
 
     def ahead(other):
         return (other < edge) & (other < turn)
@@ -221,9 +222,7 @@
     for k in range(2):
         slot = near[k]
         turned = pltpu.roll(slot, 1, 1, stride=1, stride_axis=0)
-        source = turned - 2
-        offset = ((2 * chip - (source & -2)) & (n_grp - 1)) + ((core - source) & 1)
-        index[k] = jnp.where(turned < 2, turned, 2 + offset)
+        index[k] = turned - 2
 
     for to, direct, sent in directs:
         if to >= 2:
@@ -250,11 +249,10 @@
     for to in by_turn:
         block = jnp.where(whole(lists[to]) == 0, blocks[0], blocks[1])
         block = jnp.where(whole(counts[to]) > 0, block, 0.0)
-        offset = (to // 2 - chip + chips) % chips * 2 + (to + core) % 2
         deliver_out[to, 0:SENT] = block[0:SENT]
         deliver = pltpu.make_async_remote_copy(
             src_ref=deliver_out.at[to, pl.ds(0, SENT)],
-            dst_ref=deliver_in.at[offset, pl.ds(0, SENT)],
+            dst_ref=deliver_in.at[g, pl.ds(0, SENT)],
             send_sem=deliver_send,
             recv_sem=deliver_recv,
             device_id={"grp": to},
@@ -262,12 +260,12 @@
         )
         sends = ahead(turns[to])
         if to < 2 * FRONT:
-            sends = sends & jnp.logical_not(late)
+            sends = sends & jnp.logical_not(to_front(b, to))
         pl.when(sends)(deliver.start)
         delivers.append((to, deliver))
 
     block = jnp.where(whole(lists[g]) == 0, blocks[0], blocks[1])
-    deliver_in[0] = jnp.where(whole(counts[g]) > 0, block, 0.0)
+    deliver_in[g] = jnp.where(whole(counts[g]) > 0, block, 0.0)
 
     pl.semaphore_wait(deliver_here, jnp.where(turn < edge, n_grp - 1 - early_turns, 1))
     for to in range(n_grp):
@@ -279,11 +277,13 @@
     for to, deliver in delivers:
         pl.when(jnp.logical_not(ahead(turns[to])) & (g != to))(deliver.start)
 
-    own_rows = [jnp.concatenate([blocks[k][c : c + 1] for k in (0, 1) for _ in range(4)], axis=0) for c in range(4)]
+    for k in range(2):
+        for c in range(4):
+            picked[k, c] = jnp.where(index[k] == -2, blocks[0][c : c + 1], blocks[1][c : c + 1])
     for k in range(2):
         for c in range(3):
-            row = jnp.broadcast_to(blocks[k][c : c + 1], (knb, BLOCK))
-            moved[k, c] = pltpu.roll(row, 1, 1, stride=1, stride_axis=0)
+            line = jnp.broadcast_to(blocks[k][c : c + 1], (knb, BLOCK))
+            moved[k, c] = pltpu.roll(line, 1, 1, stride=1, stride_axis=0)
 
     def delivered(ref, number):
         part = ref.at[pl.ds(1, number), pl.ds(0, SENT)]
@@ -311,20 +311,30 @@
             device_id_type=MESH,
         )
 
-    heights = 2 * FRONT * (4 * SENT + 2)
-    low_skip = (b == 0) | (second == 0)
-    high_skip = (first == 0) | (both == 0)
-    pl.when(late & jnp.logical_not(low_skip | high_skip))(directed(heights).wait_send)
-    pl.when(late & low_skip)(directed(heights - SENT - 1).wait_send)
-    pl.when(late & high_skip)(directed(heights - SENT).wait_send)
+    skip = (b == 0) | (first == 0) | (second == 0) | (both == 0)
+    for lower, more, less in ((True, 2 * SENT, SENT + 1), (False, 2 * SENT + 2, SENT)):
+        here = late & ((row < 2) if lower else (row >= 2))
+        heights = 2 * (4 * SENT + 2) + 2 * (FRONT - 1) * more
+        pl.when(here & jnp.logical_not(skip))(directed(heights).wait_send)
+        pl.when(here & skip)(directed(heights - less).wait_send)
     pl.when(jnp.logical_not(late))(delivered(deliver_out, n_grp - 1).wait_send)
-    pl.when(late)(delivered(deliver_out, n_grp - 1 - 2 * FRONT).wait_send)
+    pl.when(late & (row < 2))(delivered(deliver_out, n_grp - 3).wait_send)
+    pl.when(late & (row >= 2))(delivered(deliver_out, n_grp - 1 - 2 * FRONT).wait_send)
     pl.when(late & (b == 0))(delivered(deliver_out, 1).wait_send)
     pl.when(jnp.logical_not(front))(delivered(deliver_in, n_grp - 1).wait_recv)
 
+    pl.when(front)(delivered(deliver_in, n_grp // 2 - 1).wait_recv)
+    flat = deliver_in.reshape(n_grp * ROWS, BLOCK)
+    groups = [(k, slice(8 * v, 8 * (v + 1)), v) for k in range(2) for v in range(knb // 8)]
+    low = [flat[pl.ds(c, 8, stride=ROWS), :] for c in range(4)]
+    for k, part, v in groups:
+        source = index[k, part]
+        here = (source >= 0) & (source < 8)
+        for c in range(4):
+            picked[k, c, part] = jnp.where(here, pick(low[c], source & 7, 0), picked[k, c, part])
+
     @pl.when(front)
     def _():
-        delivered(deliver_in, n_grp // 2 - 1).wait_recv()
         directed(n_grp // 2 * (4 * SENT + 2)).wait_recv()
         for source in range(n_grp // 2):
             raw, one, two, three = (direct_in[source, kind] for kind in range(4))
@@ -332,37 +342,23 @@
             kept = jnp.broadcast_to(two[SENT : SENT + 1], (ROWS, BLOCK)) != 0.0
             block = jnp.where(code == 3.0, jnp.where(kept, two, three), jnp.where(code == 2.0, one, raw))
             block = jnp.where(code == 0.0, 0.0, block)
-            offset = 2 * (chip + chips // 2 - source // 2) + (core + source) % 2
-            deliver_in[offset, 0:SENT] = block[0:SENT]
-
-    flat = deliver_in.reshape(n_grp * ROWS, BLOCK)
-    low = [flat[pl.ds(c, 8, stride=ROWS), :] for c in range(4)]
+            deliver_in[n_grp // 2 + source, 0:SENT] = block[0:SENT]
+
     high = [flat[pl.ds(8 * ROWS + c, 8, stride=ROWS), :] for c in range(4)]
     lane = lax.broadcasted_iota(jnp.int32, (8, BLOCK), 1)
-    row = lax.broadcasted_iota(jnp.int32, (8, BLOCK), 0)
-    dist, weigh = [], []
-    for k in range(2):
-        dist_rows, mass_rows = [], []
-        for v in range(knb // 8):
-            where = index[k, 8 * v : 8 * (v + 1), :]
-            rel = where - 2
-            is_own = where < 2
-            is_low = rel < 8
-            sub = rel & 7
-            own_sub = where * 4 & 7
-            comps = []
-            for c in range(4):
-                got = jnp.where(is_low, pick_rows(low[c], sub), pick_rows(high[c], sub))
-                comps.append(jnp.where(is_own, pick_rows(own_rows[c], own_sub), got))
-            total = None
-            for c in range(3):
-                diff = comps[c] - moved[k, c, 8 * v : 8 * (v + 1), :]
-                total = diff * diff if total is None else total + diff * diff
-            back = (lane + row + (8 * v + 1)) & (BLOCK - 1)
-            dist_rows.append(pick_lanes(total, back))
-            mass_rows.append(pick_lanes(comps[3], back))
-        dist.append(jnp.concatenate(dist_rows, axis=0))
-        weigh.append(jnp.concatenate(mass_rows, axis=0))
+    dist, weigh = [[], []], [[], []]
+    for k, part, v in groups:
+        source = index[k, part]
+        comps = [jnp.where(source >= 8, pick(high[c], source & 7, 0), picked[k, c, part]) for c in range(4)]
+        total = None
+        for c in range(3):
+            diff = comps[c] - moved[k, c, part]
+            total = diff * diff if total is None else total + diff * diff
+        back = (lane + rows + (8 * v + 1)) & (BLOCK - 1)
+        dist[k].append(pick(total, back, 1))
+        weigh[k].append(pick(comps[3], back, 1))
+    dist = [jnp.concatenate(parts, axis=0) for parts in dist]
+    weigh = [jnp.concatenate(parts, axis=0) for parts in weigh]
 
     for k in range(2):
         own_mass, start = blocks[k][3:4], blocks[k][4:5]
@@ -414,6 +410,7 @@
                 pltpu.VMEM((2 * FRONT + 1, ROWS, BLOCK), f32),
                 pltpu.VMEM((n_grp // 2, 4, ROWS, BLOCK), f32),
                 pltpu.VMEM((2, 3, knb, BLOCK), f32),
+                pltpu.VMEM((2, 4, knb, BLOCK), f32),
                 pltpu.SemaphoreType.DMA((7,)),
                 pltpu.SemaphoreType.DMA,
                 pltpu.SemaphoreType.DMA,

time: 18.5 us -> 18.5 us (level)
  no operation moved by 1% of the time
where the time goes in v7:
time: 18.5 us; the launch traced here: 18.3 us
  Pallas kernels  17.1 us (92%)
  between operations  0.64 us (3%)
  other arithmetic  0.57 us (3%)
    pallas_call x1, Pallas kernels, on_device(): pl.pallas_call(lambda *refs: kernel(n_grp, n_bis, knb, *refs), name='sett...  17.1 us
    reshape x1, other arithmetic, on_device(): return (length.reshape(-1), density.reshape(-1))  0.57 us

profile of v7, /device:TPU:1, one launch (start us, length us, event | category | flops | bytes accessed | tf_op | source)
XLA Modules:
  0.0 18.3 jit_solution(1840575676721545517)
XLA Ops:
  0.6 17.1 %settle.1 = (f32[2,128]{1,0:T(2,128)S(1)}, f32[2,128]{1,0:T(2,128)S(1)}) custom-call(f32[3,256]{1,0:T(4,128)} %refs_0_.1, f32[2,128]{1,0:T(2,128)} %bitcast.9, f32[2,128]{1,0:T(2,128)} %bitcast.10, s32[2]{0:T(128)} %bitcast.11, s32[16]{0:T(128)} %bitcast.12, s32[16]{0:T(128)} %bitcast.13, s32[2,64,128]{2,1,0:T(8,128)} %refs_6_.1), custom_call_target="tpu_custom_call" | custom-call | tf_op jit(solution)/shard_map/settle/pallas_call | solution.py:390
  17.8 0.6 %fusion.1 = (f32[256]{0:T(256)}, f32[256]{0:T(256)}) fusion(f32[2,128]{1,0:T(2,128)S(1)} %get-tuple-element.5, f32[2,128]{1,0:T(2,128)S(1)} %get-tuple-element.4), kind=kLoop, calls=%fused_computation.2 | loop fusion | flops 1280 | bytes 4096 | tf_op jit(solution)/shard_map/reshape | solution.py:440

commit v8 on v7

--- a/solution.py
+++ b/solution.py
@@ -140,22 +140,6 @@
             for to in late_devices:
                 pl.semaphore_signal(barrier, inc=1, device_id={"bis": partner, "grp": to}, device_id_type=MESH)
 
-    @pl.when(announced > 0)
-    def _():
-        pl.semaphore_wait(barrier, announced)
-
-    for i, (partner, other) in enumerate(zip(trade_with, row_turns)):
-
-        @pl.when(other < row_turn)
-        def _():
-            pl.semaphore_signal(trade_here.at[i], inc=1, device_id={"bis": partner}, device_id_type=MESH)
-
-    for to in by_turn:
-
-        @pl.when(ahead(turns[to]))
-        def _():
-            pl.semaphore_signal(deliver_here, inc=1, device_id={"grp": to}, device_id_type=MESH)
-
     for load in loads[:-1]:
         load.wait()
 
@@ -170,6 +154,14 @@
     trade_out[0] = jnp.where(whole(l0) == 0, blocks[0], blocks[1])
     trade_out[1] = jnp.where(whole(l1) == 0, blocks[0], blocks[1])
 
+    place = (chip - chips // 2) * 2 + core
+    rows = lax.broadcasted_iota(jnp.int32, (ROWS, BLOCK), 0)
+    direct_out[2 * FRONT] = jnp.where(rows == SENT, jnp.broadcast_to(flag, (ROWS, BLOCK)), trade_out[1])
+    for to in front_devices:
+        chosen = whole(lists[to])
+        code = jnp.where(chosen == l1, 3.0, jnp.where(chosen == l0, 2.0, 1.0))
+        code = jnp.where(whole(counts[to]) > 0, code, 0.0)
+        direct_out[to] = jnp.where(rows == SENT, code, jnp.where(chosen == 0, blocks[0], blocks[1]))
     trades = [
         pltpu.make_async_remote_copy(
             src_ref=trade_out.at[src, pl.ds(0, 6)],
@@ -181,16 +173,12 @@
         )
         for src, dst, partner in ((0, 0, first), (1, 1, second), (0, 2, both))
     ]
+    @pl.when(announced > 0)
+    def _():
+        pl.semaphore_wait(barrier, announced)
+
     for trade, other in zip(trades, row_turns):
         pl.when(other < row_turn)(trade.start)
-    place = (chip - chips // 2) * 2 + core
-    rows = lax.broadcasted_iota(jnp.int32, (ROWS, BLOCK), 0)
-    direct_out[2 * FRONT] = jnp.where(rows == SENT, jnp.broadcast_to(flag, (ROWS, BLOCK)), trade_out[1])
-    for to in front_devices:
-        chosen = whole(lists[to])
-        code = jnp.where(chosen == l1, 3.0, jnp.where(chosen == l0, 2.0, 1.0))
-        code = jnp.where(whole(counts[to]) > 0, code, 0.0)
-        direct_out[to] = jnp.where(rows == SENT, code, jnp.where(chosen == 0, blocks[0], blocks[1]))
     directs = []
     for to in front_devices:
         for src, kind, height, partner in (
@@ -211,6 +199,18 @@
     for to, direct, sent in directs:
         if to < 2:
             pl.when(sent)(direct.start)
+    for i, (partner, other) in enumerate(zip(trade_with, row_turns)):
+
+        @pl.when(other < row_turn)
+        def _():
+            pl.semaphore_signal(trade_here.at[i], inc=1, device_id={"bis": partner}, device_id_type=MESH)
+
+    for to in by_turn:
+
+        @pl.when(ahead(turns[to]))
+        def _():
+            pl.semaphore_signal(deliver_here, inc=1, device_id={"grp": to}, device_id_type=MESH)
+
     for i in (1, 2, 0):
 
         @pl.when(row_turns[i] > row_turn)

time: 18.5 us -> 18.4 us (level)
  no operation moved by 1% of the time
where the time goes in v8:
time: 18.4 us; the launch traced here: 18.3 us
  Pallas kernels  17.1 us (93%)
  between operations  0.64 us (3%)
  other arithmetic  0.57 us (3%)
    pallas_call x1, Pallas kernels, on_device(): pl.pallas_call(lambda *refs: kernel(n_grp, n_bis, knb, *refs), name='sett...  17.1 us
    reshape x1, other arithmetic, on_device(): return (length.reshape(-1), density.reshape(-1))  0.57 us

profile of v8, /device:TPU:1, one launch (start us, length us, event | category | flops | bytes accessed | tf_op | source)
XLA Modules:
  0.0 18.3 jit_solution(11518628230802324916)
XLA Ops:
  0.6 17.1 %settle.1 = (f32[2,128]{1,0:T(2,128)S(1)}, f32[2,128]{1,0:T(2,128)S(1)}) custom-call(f32[3,256]{1,0:T(4,128)} %refs_0_.1, f32[2,128]{1,0:T(2,128)} %bitcast.9, f32[2,128]{1,0:T(2,128)} %bitcast.10, s32[2]{0:T(128)} %bitcast.11, s32[16]{0:T(128)} %bitcast.12, s32[16]{0:T(128)} %bitcast.13, s32[2,64,128]{2,1,0:T(8,128)} %refs_6_.1), custom_call_target="tpu_custom_call" | custom-call | tf_op jit(solution)/shard_map/settle/pallas_call | solution.py:390
  17.7 0.6 %fusion.1 = (f32[256]{0:T(256)}, f32[256]{0:T(256)}) fusion(f32[2,128]{1,0:T(2,128)S(1)} %get-tuple-element.5, f32[2,128]{1,0:T(2,128)S(1)} %get-tuple-element.4), kind=kLoop, calls=%fused_computation.2 | loop fusion | flops 1280 | bytes 4096 | tf_op jit(solution)/shard_map/reshape | solution.py:440

commit v9 on v8

--- a/solution.py
+++ b/solution.py
@@ -108,15 +108,15 @@
     by_turn = [to ^ 1 for to in range(n_grp)]
 
     late = chip >= chips // 2
-    front = (turn < edge) & ((chip == 0) | ((chip < FRONT) & (row >= 2)))
+    front = (turn < edge) & ((chip < 2) | ((chip < FRONT) & (row >= 2)))
     late_devices = range(n_grp // 2, n_grp)
     front_devices = [to ^ 1 for to in range(2 * FRONT)]
-    fronts = 6 - sum(jnp.where(partner == 0, 1, 0) for partner in trade_with)
-    fronts = fronts + 2 * (FRONT - 1) * jnp.where(row < 2, 2, 1)
+    fronts = 12 - sum(jnp.where(partner == 0, 1, 0) for partner in trade_with)
+    fronts = fronts + 2 * (FRONT - 2) * jnp.where(row < 2, 2, 1)
     announced = early_turns + row_turn + jnp.where(late, fronts, 0)
 
     def to_front(partner, to):
-        return late & ((partner + to > 0) if to < 2 else (partner >= half))
+        return late & ((partner + to > 0) if to < 4 else (partner >= half))
 
     def ahead(other):
         return (other < edge) & (other < turn)
@@ -314,11 +314,11 @@
     skip = (b == 0) | (first == 0) | (second == 0) | (both == 0)
     for lower, more, less in ((True, 2 * SENT, SENT + 1), (False, 2 * SENT + 2, SENT)):
         here = late & ((row < 2) if lower else (row >= 2))
-        heights = 2 * (4 * SENT + 2) + 2 * (FRONT - 1) * more
+        heights = 4 * (4 * SENT + 2) + 2 * (FRONT - 2) * more
         pl.when(here & jnp.logical_not(skip))(directed(heights).wait_send)
         pl.when(here & skip)(directed(heights - less).wait_send)
     pl.when(jnp.logical_not(late))(delivered(deliver_out, n_grp - 1).wait_send)
-    pl.when(late & (row < 2))(delivered(deliver_out, n_grp - 3).wait_send)
+    pl.when(late & (row < 2))(delivered(deliver_out, n_grp - 5).wait_send)
     pl.when(late & (row >= 2))(delivered(deliver_out, n_grp - 1 - 2 * FRONT).wait_send)
     pl.when(late & (b == 0))(delivered(deliver_out, 1).wait_send)
     pl.when(jnp.logical_not(front))(delivered(deliver_in, n_grp - 1).wait_recv)

time: 18.4 us -> 18.5 us (level)
  no operation moved by 1% of the time
where the time goes in v9:
time: 18.5 us; the launch traced here: 18.4 us
  Pallas kernels  17.2 us (93%)
  between operations  0.64 us (3%)
  other arithmetic  0.57 us (3%)
    pallas_call x1, Pallas kernels, on_device(): pl.pallas_call(lambda *refs: kernel(n_grp, n_bis, knb, *refs), name='sett...  17.2 us
    reshape x1, other arithmetic, on_device(): return (length.reshape(-1), density.reshape(-1))  0.57 us

profile of v9, /device:TPU:1, one launch (start us, length us, event | category | flops | bytes accessed | tf_op | source)
XLA Modules:
  0.0 18.4 jit_solution(15904900468491930502)
XLA Ops:
  0.6 17.2 %settle.1 = (f32[2,128]{1,0:T(2,128)S(1)}, f32[2,128]{1,0:T(2,128)S(1)}) custom-call(f32[3,256]{1,0:T(4,128)} %refs_0_.1, f32[2,128]{1,0:T(2,128)} %bitcast.9, f32[2,128]{1,0:T(2,128)} %bitcast.10, s32[2]{0:T(128)} %bitcast.11, s32[16]{0:T(128)} %bitcast.12, s32[16]{0:T(128)} %bitcast.13, s32[2,64,128]{2,1,0:T(8,128)} %refs_6_.1), custom_call_target="tpu_custom_call" | custom-call | tf_op jit(solution)/shard_map/settle/pallas_call | solution.py:390
  17.8 0.6 %fusion.1 = (f32[256]{0:T(256)}, f32[256]{0:T(256)}) fusion(f32[2,128]{1,0:T(2,128)S(1)} %get-tuple-element.5, f32[2,128]{1,0:T(2,128)S(1)} %get-tuple-element.4), kind=kLoop, calls=%fused_computation.2 | loop fusion | flops 1280 | bytes 4096 | tf_op jit(solution)/shard_map/reshape | solution.py:440

commit v10 on v9

--- a/solution.py
+++ b/solution.py
@@ -10,7 +10,7 @@
 BLOCK = 128
 ROWS = 8
 SENT = 4
-FRONT = 3
+FRONT = 2
 ITERS = 3
 TARGET = 16.0
 NORM = math.pi**-1.5
@@ -108,15 +108,14 @@
     by_turn = [to ^ 1 for to in range(n_grp)]
 
     late = chip >= chips // 2
-    front = (turn < edge) & ((chip < 2) | ((chip < FRONT) & (row >= 2)))
+    front = (turn < edge) & (chip < FRONT)
     late_devices = range(n_grp // 2, n_grp)
     front_devices = [to ^ 1 for to in range(2 * FRONT)]
-    fronts = 12 - sum(jnp.where(partner == 0, 1, 0) for partner in trade_with)
-    fronts = fronts + 2 * (FRONT - 2) * jnp.where(row < 2, 2, 1)
+    fronts = 6 * FRONT - sum(jnp.where(partner == 0, 1, 0) for partner in trade_with)
     announced = early_turns + row_turn + jnp.where(late, fronts, 0)
 
     def to_front(partner, to):
-        return late & ((partner + to > 0) if to < 4 else (partner >= half))
+        return late & (partner + to > 0)
 
     def ahead(other):
         return (other < edge) & (other < turn)
@@ -311,15 +310,14 @@
             device_id_type=MESH,
         )
 
-    skip = (b == 0) | (first == 0) | (second == 0) | (both == 0)
-    for lower, more, less in ((True, 2 * SENT, SENT + 1), (False, 2 * SENT + 2, SENT)):
-        here = late & ((row < 2) if lower else (row >= 2))
-        heights = 4 * (4 * SENT + 2) + 2 * (FRONT - 2) * more
-        pl.when(here & jnp.logical_not(skip))(directed(heights).wait_send)
-        pl.when(here & skip)(directed(heights - less).wait_send)
+    heights = 2 * FRONT * (4 * SENT + 2)
+    low_skip = (b == 0) | (second == 0)
+    high_skip = (first == 0) | (both == 0)
+    pl.when(late & jnp.logical_not(low_skip | high_skip))(directed(heights).wait_send)
+    pl.when(late & low_skip)(directed(heights - SENT - 1).wait_send)
+    pl.when(late & high_skip)(directed(heights - SENT).wait_send)
     pl.when(jnp.logical_not(late))(delivered(deliver_out, n_grp - 1).wait_send)
-    pl.when(late & (row < 2))(delivered(deliver_out, n_grp - 5).wait_send)
-    pl.when(late & (row >= 2))(delivered(deliver_out, n_grp - 1 - 2 * FRONT).wait_send)
+    pl.when(late)(delivered(deliver_out, n_grp - 1 - 2 * FRONT).wait_send)
     pl.when(late & (b == 0))(delivered(deliver_out, 1).wait_send)
     pl.when(jnp.logical_not(front))(delivered(deliver_in, n_grp - 1).wait_recv)
 

time: 18.5 us -> 18.4 us (level)
  Pallas kernels: 17.2 us -> 17 us
where the time goes in v10:
time: 18.4 us; the launch traced here: 18.2 us
  Pallas kernels  17 us (92%)
  between operations  0.64 us (3%)
  other arithmetic  0.57 us (3%)
    pallas_call x1, Pallas kernels, on_device(): pl.pallas_call(lambda *refs: kernel(n_grp, n_bis, knb, *refs), name='sett...  17 us
    reshape x1, other arithmetic, on_device(): return (length.reshape(-1), density.reshape(-1))  0.57 us

profile of v10, /device:TPU:1, one launch (start us, length us, event | category | flops | bytes accessed | tf_op | source)
XLA Modules:
  0.0 18.2 jit_solution(2931392451512817729)
XLA Ops:
  0.6 17.0 %settle.1 = (f32[2,128]{1,0:T(2,128)S(1)}, f32[2,128]{1,0:T(2,128)S(1)}) custom-call(f32[3,256]{1,0:T(4,128)} %refs_0_.1, f32[2,128]{1,0:T(2,128)} %bitcast.9, f32[2,128]{1,0:T(2,128)} %bitcast.10, s32[2]{0:T(128)} %bitcast.11, s32[16]{0:T(128)} %bitcast.12, s32[16]{0:T(128)} %bitcast.13, s32[2,64,128]{2,1,0:T(8,128)} %refs_6_.1), custom_call_target="tpu_custom_call" | custom-call | tf_op jit(solution)/shard_map/settle/pallas_call | solution.py:388
  17.7 0.6 %fusion.1 = (f32[256]{0:T(256)}, f32[256]{0:T(256)}) fusion(f32[2,128]{1,0:T(2,128)S(1)} %get-tuple-element.5, f32[2,128]{1,0:T(2,128)S(1)} %get-tuple-element.4), kind=kLoop, calls=%fused_computation.2 | loop fusion | flops 1280 | bytes 4096 | tf_op jit(solution)/shard_map/reshape | solution.py:438

commit v11 on v10

--- a/solution.py
+++ b/solution.py
@@ -60,11 +60,9 @@
     moved,
     picked,
     load_sem,
-    trade_send,
+    sent_sem,
     trade_recv,
-    deliver_send,
     deliver_recv,
-    direct_send,
     direct_recv,
     trade_here,
     deliver_here,
@@ -80,7 +78,7 @@
     chip, core = g // 2, g % 2
 
     loads = [
-        pltpu.make_async_copy(src, dst, load_sem.at[i])
+        pltpu.make_async_copy(src, dst, load_sem.at[i // 6])
         for i, (src, dst) in enumerate(
             [
                 (swap_hbm, swap),
@@ -165,7 +163,7 @@
         pltpu.make_async_remote_copy(
             src_ref=trade_out.at[src, pl.ds(0, 6)],
             dst_ref=trade_in.at[dst, pl.ds(0, 6)],
-            send_sem=trade_send,
+            send_sem=sent_sem,
             recv_sem=trade_recv,
             device_id={"bis": partner},
             device_id_type=MESH,
@@ -189,7 +187,7 @@
             direct = pltpu.make_async_remote_copy(
                 src_ref=src.at[pl.ds(0, height)],
                 dst_ref=direct_in.at[place, kind, pl.ds(0, height)],
-                send_sem=direct_send,
+                send_sem=sent_sem,
                 recv_sem=direct_recv,
                 device_id={"bis": partner, "grp": to},
                 device_id_type=MESH,
@@ -230,7 +228,7 @@
     pltpu.make_async_remote_copy(
         src_ref=trade_in.at[:, pl.ds(0, 6)],
         dst_ref=trade_in.at[:, pl.ds(0, 6)],
-        send_sem=trade_send,
+        send_sem=sent_sem,
         recv_sem=trade_recv,
         device_id={"bis": first},
         device_id_type=MESH,
@@ -252,7 +250,7 @@
         deliver = pltpu.make_async_remote_copy(
             src_ref=deliver_out.at[to, pl.ds(0, SENT)],
             dst_ref=deliver_in.at[g, pl.ds(0, SENT)],
-            send_sem=deliver_send,
+            send_sem=sent_sem,
             recv_sem=deliver_recv,
             device_id={"grp": to},
             device_id_type=MESH,
@@ -289,7 +287,7 @@
         return pltpu.make_async_remote_copy(
             src_ref=part,
             dst_ref=part,
-            send_sem=deliver_send,
+            send_sem=sent_sem,
             recv_sem=deliver_recv,
             device_id={"grp": g},
             device_id_type=MESH,
@@ -304,7 +302,7 @@
         return pltpu.make_async_remote_copy(
             src_ref=part,
             dst_ref=part,
-            send_sem=direct_send,
+            send_sem=sent_sem,
             recv_sem=direct_recv,
             device_id={"grp": g},
             device_id_type=MESH,
@@ -409,9 +407,7 @@
                 pltpu.VMEM((n_grp // 2, 4, ROWS, BLOCK), f32),
                 pltpu.VMEM((2, 3, knb, BLOCK), f32),
                 pltpu.VMEM((2, 4, knb, BLOCK), f32),
-                pltpu.SemaphoreType.DMA((7,)),
-                pltpu.SemaphoreType.DMA,
-                pltpu.SemaphoreType.DMA,
+                pltpu.SemaphoreType.DMA((2,)),
                 pltpu.SemaphoreType.DMA,
                 pltpu.SemaphoreType.DMA,
                 pltpu.SemaphoreType.DMA,

time: 18.4 us -> 18.3 us (level)
  no operation moved by 1% of the time
where the time goes in v11:
time: 18.3 us; the launch traced here: 18.2 us
  Pallas kernels  17 us (93%)
  between operations  0.64 us (3%)
  other arithmetic  0.57 us (3%)
    pallas_call x1, Pallas kernels, on_device(): pl.pallas_call(lambda *refs: kernel(n_grp, n_bis, knb, *refs), name='sett...  17 us
    reshape x1, other arithmetic, on_device(): return (length.reshape(-1), density.reshape(-1))  0.57 us

profile of v11, /device:TPU:1, one launch (start us, length us, event | category | flops | bytes accessed | tf_op | source)
XLA Modules:
  0.0 18.2 jit_solution(12810672803904722846)
XLA Ops:
  0.6 17.0 %settle.1 = (f32[2,128]{1,0:T(2,128)S(1)}, f32[2,128]{1,0:T(2,128)S(1)}) custom-call(f32[3,256]{1,0:T(4,128)} %refs_0_.1, f32[2,128]{1,0:T(2,128)} %bitcast.9, f32[2,128]{1,0:T(2,128)} %bitcast.10, s32[2]{0:T(128)} %bitcast.11, s32[16]{0:T(128)} %bitcast.12, s32[16]{0:T(128)} %bitcast.13, s32[2,64,128]{2,1,0:T(8,128)} %refs_6_.1), custom_call_target="tpu_custom_call" | custom-call | tf_op jit(solution)/shard_map/settle/pallas_call | solution.py:386
  17.6 0.6 %fusion.1 = (f32[256]{0:T(256)}, f32[256]{0:T(256)}) fusion(f32[2,128]{1,0:T(2,128)S(1)} %get-tuple-element.5, f32[2,128]{1,0:T(2,128)S(1)} %get-tuple-element.4), kind=kLoop, calls=%fused_computation.2 | loop fusion | flops 1280 | bytes 4096 | tf_op jit(solution)/shard_map/reshape | solution.py:434

commit v12 on v11

--- a/solution.py
+++ b/solution.py
@@ -208,9 +208,9 @@
         def _():
             pl.semaphore_signal(deliver_here, inc=1, device_id={"grp": to}, device_id_type=MESH)
 
-    for i in (1, 2, 0):
-
-        @pl.when(row_turns[i] > row_turn)
+    for i, now in ((1, row >= 0), (0, row == 1), (2, row >= 0), (0, row != 1)):
+
+        @pl.when((row_turns[i] > row_turn) & now)
         def _():
             pl.semaphore_wait(trade_here.at[i], 1)
             trades[i].start()

time: 18.3 us -> 18.3 us (level)
  no operation moved by 1% of the time
where the time goes in v12:
time: 18.3 us; the launch traced here: 18.2 us
  Pallas kernels  17 us (93%)
  between operations  0.64 us (3%)
  other arithmetic  0.57 us (3%)
    pallas_call x1, Pallas kernels, on_device(): pl.pallas_call(lambda *refs: kernel(n_grp, n_bis, knb, *refs), name='sett...  17 us
    reshape x1, other arithmetic, on_device(): return (length.reshape(-1), density.reshape(-1))  0.57 us

profile of v12, /device:TPU:1, one launch (start us, length us, event | category | flops | bytes accessed | tf_op | source)
XLA Modules:
  0.0 18.2 jit_solution(273225328553961057)
XLA Ops:
  0.6 17.0 %settle.1 = (f32[2,128]{1,0:T(2,128)S(1)}, f32[2,128]{1,0:T(2,128)S(1)}) custom-call(f32[3,256]{1,0:T(4,128)} %refs_0_.1, f32[2,128]{1,0:T(2,128)} %bitcast.9, f32[2,128]{1,0:T(2,128)} %bitcast.10, s32[2]{0:T(128)} %bitcast.11, s32[16]{0:T(128)} %bitcast.12, s32[16]{0:T(128)} %bitcast.13, s32[2,64,128]{2,1,0:T(8,128)} %refs_6_.1), custom_call_target="tpu_custom_call" | custom-call | tf_op jit(solution)/shard_map/settle/pallas_call | solution.py:386
  17.6 0.6 %fusion.1 = (f32[256]{0:T(256)}, f32[256]{0:T(256)}) fusion(f32[2,128]{1,0:T(2,128)S(1)} %get-tuple-element.5, f32[2,128]{1,0:T(2,128)S(1)} %get-tuple-element.4), kind=kLoop, calls=%fused_computation.2 | loop fusion | flops 1280 | bytes 4096 | tf_op jit(solution)/shard_map/reshape | solution.py:434

commit v13 on v11

--- a/solution.py
+++ b/solution.py
@@ -240,7 +240,6 @@
     for k in range(2):
         block = jnp.where(whole(l0) == k, from_first, blocks[k])
         blocks[k] = jnp.where(whole(l1) == k, from_second, block)
-        final[k] = blocks[k]
 
     delivers = []
     for to in by_turn:
@@ -281,6 +280,8 @@
         for c in range(3):
             line = jnp.broadcast_to(blocks[k][c : c + 1], (knb, BLOCK))
             moved[k, c] = pltpu.roll(line, 1, 1, stride=1, stride_axis=0)
+
+    starts = [(block[3:4], jnp.log(TARGET * block[3:4]), 1.0 / block[4:5]) for block in blocks]
 
     def delivered(ref, number):
         part = ref.at[pl.ds(1, number), pl.ds(0, SENT)]
@@ -357,9 +358,7 @@
     weigh = [jnp.concatenate(parts, axis=0) for parts in weigh]
 
     for k in range(2):
-        own_mass, start = blocks[k][3:4], blocks[k][4:5]
-        log_target = jnp.log(TARGET * own_mass)
-        inverse = 1.0 / start
+        own_mass, log_target, inverse = starts[k]
         for step in range(ITERS):
             narrow = inverse * inverse
             weight = weigh[k] * jnp.exp2(dist[k] * (narrow * -LOG2E))

time: 18.3 us -> 18.3 us (level)
  no operation moved by 1% of the time
where the time goes in v13:
time: 18.3 us; the launch traced here: 18.2 us
  Pallas kernels  17 us (93%)
  between operations  0.64 us (3%)
  other arithmetic  0.57 us (3%)
    pallas_call x1, Pallas kernels, on_device(): pl.pallas_call(lambda *refs: kernel(n_grp, n_bis, knb, *refs), name='sett...  17 us
    reshape x1, other arithmetic, on_device(): return (length.reshape(-1), density.reshape(-1))  0.57 us

profile of v13, /device:TPU:1, one launch (start us, length us, event | category | flops | bytes accessed | tf_op | source)
XLA Modules:
  0.0 18.2 jit_solution(8138225533658175568)
XLA Ops:
  0.6 17.0 %settle.1 = (f32[2,128]{1,0:T(2,128)S(1)}, f32[2,128]{1,0:T(2,128)S(1)}) custom-call(f32[3,256]{1,0:T(4,128)} %refs_0_.1, f32[2,128]{1,0:T(2,128)} %bitcast.9, f32[2,128]{1,0:T(2,128)} %bitcast.10, s32[2]{0:T(128)} %bitcast.11, s32[16]{0:T(128)} %bitcast.12, s32[16]{0:T(128)} %bitcast.13, s32[2,64,128]{2,1,0:T(8,128)} %refs_6_.1), custom_call_target="tpu_custom_call" | custom-call | tf_op jit(solution)/shard_map/settle/pallas_call | solution.py:385
  17.6 0.6 %fusion.1 = (f32[256]{0:T(256)}, f32[256]{0:T(256)}) fusion(f32[2,128]{1,0:T(2,128)S(1)} %get-tuple-element.5, f32[2,128]{1,0:T(2,128)S(1)} %get-tuple-element.4), kind=kLoop, calls=%fused_computation.2 | loop fusion | flops 1280 | bytes 4096 | tf_op jit(solution)/shard_map/reshape | solution.py:433
